TPU v7x, 256 devices: a whole 4x4x8 slice. The times are simulated.
256 devices in a mesh: ctx: 64 (over x, z, core), tp: 4 (over y).
Axes of the slice: x: 4, y: 4, z: 8, core: 2. Of those that a mesh axis runs over, the one named last changes fastest.
Arguments:
- tokens: bfloat16 [8192, 4096], P('ctx', 'tp'), may hold values from -70 to 70
- norm_gain: float32 [4096], P('tp'), may hold values from 0.5 to 1.5
- short_filter: float32 [3, 3, 4096], P(None, None, 'tp'), may hold values from -3.6 to 3.6
- medium_filter: float32 [128, 4096], P(None, 'tp'), may hold values from -0.5 to 0.5
- residues: float32 [4096, 16], P(('tp', 'ctx')), may hold values from -2.1 to 2.1
- decay_rate: float32 [4096, 16], P(('tp', 'ctx')), may hold values from 0.5 to 500
- skip_gain: float32 [4096], P(('tp', 'ctx')), may hold values from -4 to 4
- grad_out: bfloat16 [8192, 4096], P('ctx', 'tp'), may hold values from -6 to 6
Outputs:
- block_out: bfloat16 [8192, 4096], P('ctx', 'tp')
- grad_tokens: bfloat16 [8192, 4096], P('ctx', 'tp')
- grad_gain: float32 [4096], P('tp')
- grad_short: float32 [3, 3, 4096], P(None, None, 'tp')
- grad_medium: float32 [128, 4096], P(None, 'tp')
- grad_skip: float32 [4096], P(('tp', 'ctx'))
- grad_residues: float32 [4096, 16], P(('tp', 'ctx'))
- grad_decay: float32 [4096, 16], P(('tp', 'ctx'))
All inputs are finite; a program needn't handle non-finite values.
Results may differ from a plain program's by a relative error of at most 0.0077.
Values may be sent and summed in bfloat16 or wider, within the bound.
A program may use at most 64 MiB of HBM per device.

v0:
```python
import math

import jax
import jax.numpy as jnp
from jax import lax
from jax.sharding import PartitionSpec as P

EPSILON = 1e-06
HIGHEST = lax.Precision.HIGHEST
radix_cols = 128


def from_behind(shard, axis, by):
    devices = lax.axis_size(axis)
    pairs = [(i, i + by) for i in range(devices) if 0 <= i + by < devices]
    return lax.ppermute(shard, axis, pairs)


def depthwise(extended, weights):
    result = lax.conv_general_dilated(
        extended[None],
        weights[:, None, :],
        (1,),
        "VALID",
        dimension_numbers=("NWC", "WIO", "NWC"),
        feature_group_count=extended.shape[1],
        precision=HIGHEST,
    )
    return result[0]


def angle_tables(count, other, period):
    first_index = lax.broadcasted_iota(jnp.int32, (count, other), 0)
    second_index = lax.broadcasted_iota(jnp.int32, (count, other), 1)
    angles = (first_index * second_index % period).astype(jnp.float32) * (2.0 * math.pi / period)
    return (jnp.cos(angles), jnp.sin(angles))


def contract(pattern, operand, matrix):
    return jnp.einsum(
        pattern, operand, matrix, precision=HIGHEST, preferred_element_type=jnp.float32
    )


def forward_spectrum(signal):
    channels = signal.shape[0]
    length = signal.shape[1]
    period = 2 * length
    spectrum_rows = period // radix_cols
    half_rows = spectrum_rows // 2
    blocked = signal.reshape(channels, half_rows, radix_cols)
    cos_outer, sin_outer = angle_tables(half_rows, spectrum_rows, spectrum_rows)
    section_real = contract("cab,ak->ckb", blocked, cos_outer)
    section_imag = -contract("cab,ak->ckb", blocked, sin_outer)
    cos_twist, sin_twist = angle_tables(spectrum_rows, radix_cols, period)
    twist_real = section_real * cos_twist + section_imag * sin_twist
    twist_imag = section_imag * cos_twist - section_real * sin_twist
    cos_inner, sin_inner = angle_tables(radix_cols, radix_cols, radix_cols)
    spec_real = contract("ckb,bm->ckm", twist_real, cos_inner) + contract(
        "ckb,bm->ckm", twist_imag, sin_inner
    )
    spec_imag = contract("ckb,bm->ckm", twist_imag, cos_inner) - contract(
        "ckb,bm->ckm", twist_real, sin_inner
    )
    return (spec_real, spec_imag)


def inverse_spectrum(spec_real, spec_imag):
    channels = spec_real.shape[0]
    spectrum_rows = spec_real.shape[1]
    period = spectrum_rows * radix_cols
    half_rows = spectrum_rows // 2
    cos_inner, sin_inner = angle_tables(radix_cols, radix_cols, radix_cols)
    mid_real = contract("ckm,mb->ckb", spec_real, cos_inner) - contract(
        "ckm,mb->ckb", spec_imag, sin_inner
    )
    mid_imag = contract("ckm,mb->ckb", spec_imag, cos_inner) + contract(
        "ckm,mb->ckb", spec_real, sin_inner
    )
    cos_twist, sin_twist = angle_tables(spectrum_rows, radix_cols, period)
    twist_real = mid_real * cos_twist - mid_imag * sin_twist
    twist_imag = mid_imag * cos_twist + mid_real * sin_twist
    cos_outer, sin_outer = angle_tables(spectrum_rows, half_rows, spectrum_rows)
    result = contract("ckb,ka->cab", twist_real, cos_outer) - contract(
        "ckb,ka->cab", twist_imag, sin_outer
    )
    return result.reshape(channels, half_rows * radix_cols) / period


def long_forward(signal, residues, decay_rate, skip_gain):
    length = signal.shape[1]
    mode_rates = decay_rate / length
    mode_roots = jnp.sqrt(mode_rates)
    positions = jnp.arange(length, dtype=jnp.int32).astype(jnp.float32)
    kernel = jnp.zeros(signal.shape, jnp.float32)
    for mode_index in range(residues.shape[1]):
        weight_now = residues[:, mode_index] * mode_roots[:, mode_index]
        kernel = kernel + weight_now[:, None] * jnp.exp(
            -mode_rates[:, mode_index, None] * positions
        )
    widened = signal.astype(jnp.float32)
    sig_real, sig_imag = forward_spectrum(widened)
    ker_real, ker_imag = forward_spectrum(kernel)
    conv_part = inverse_spectrum(
        sig_real * ker_real - sig_imag * ker_imag, sig_real * ker_imag + sig_imag * ker_real
    )
    result = (conv_part + skip_gain[:, None] * widened).astype(jnp.bfloat16)
    return (result, (widened, sig_real, sig_imag, ker_real, ker_imag))


def long_backward(grad_cols, saved, residues, decay_rate, skip_gain):
    widened, sig_real, sig_imag, ker_real, ker_imag = saved
    length = grad_cols.shape[1]
    mode_rates = decay_rate / length
    mode_roots = jnp.sqrt(mode_rates)
    positions = jnp.arange(length, dtype=jnp.int32).astype(jnp.float32)
    grad_wide = grad_cols.astype(jnp.float32)
    grad_real, grad_imag = forward_spectrum(grad_wide)
    back_part = inverse_spectrum(
        ker_real * grad_real + ker_imag * grad_imag, ker_real * grad_imag - ker_imag * grad_real
    )
    back_cols = (back_part + skip_gain[:, None] * grad_wide).astype(jnp.bfloat16)
    kernel_grad = inverse_spectrum(
        sig_real * grad_real + sig_imag * grad_imag, sig_real * grad_imag - sig_imag * grad_real
    )
    grad_skip = jnp.sum(grad_wide * widened, axis=1)
    first_list = []
    second_list = []
    for mode_index in range(residues.shape[1]):
        decayed = kernel_grad * jnp.exp(-mode_rates[:, mode_index, None] * positions)
        first_list.append(jnp.sum(decayed, axis=1))
        second_list.append(jnp.sum(decayed * positions, axis=1))
    first_sum = jnp.stack(first_list, 1)
    second_sum = jnp.stack(second_list, 1)
    grad_residues = mode_roots * first_sum
    grad_decay = residues / length * (first_sum / (2.0 * mode_roots) - mode_roots * second_sum)
    return (back_cols, grad_skip, grad_residues, grad_decay)


def per_device(
    tokens, norm_gain, short_filter, medium_filter, residues, decay_rate, skip_gain, grad_out
):
    tok_rows = tokens.shape[0]
    channels = tokens.shape[1]
    short_taps = short_filter.shape[1]
    long_taps = medium_filter.shape[0]
    total_chans = channels * lax.axis_size("tp")
    widened = tokens.astype(jnp.float32)
    squares = lax.psum(jnp.sum(widened * widened, axis=1), "tp")
    inv_rms = lax.rsqrt(squares / total_chans + EPSILON)
    normed = (widened * inv_rms[:, None] * norm_gain).astype(jnp.bfloat16)
    filter_bank = short_filter.transpose(1, 0, 2).reshape(short_taps, 3 * channels)
    rim_before = from_behind(normed[tok_rows - short_taps + 1 :], "ctx", 1)
    normed_window = jnp.concatenate([rim_before, normed], 0).astype(jnp.float32)
    mixed_rows = depthwise(jnp.tile(normed_window, (1, 3)), filter_bank[::-1])
    query_rows = mixed_rows[:, :channels]
    key_rows = mixed_rows[:, channels : 2 * channels]
    value_rows = mixed_rows[:, 2 * channels :]
    gated = (key_rows * value_rows).astype(jnp.bfloat16)
    gated_before = from_behind(gated[tok_rows - long_taps + 1 :], "ctx", 1)
    gated_ext = jnp.concatenate([gated_before, gated], 0)
    gated_wide = gated_ext.astype(jnp.float32)
    signal = depthwise(gated_wide, medium_filter[::-1]).astype(jnp.bfloat16)
    grad_gate = (grad_out.astype(jnp.float32) * query_rows).astype(jnp.bfloat16)
    signal_cols = lax.all_to_all(signal.T, "ctx", split_axis=0, concat_axis=1, tiled=True)
    conv_cols, saved = long_forward(signal_cols, residues, decay_rate, skip_gain)
    conv_back = lax.all_to_all(conv_cols, "ctx", split_axis=1, concat_axis=0, tiled=True)
    grad_cols = lax.all_to_all(grad_gate.T, "ctx", split_axis=0, concat_axis=1, tiled=True)
    back_cols, grad_skip, grad_residues, grad_decay = long_backward(
        grad_cols, saved, residues, decay_rate, skip_gain
    )
    back_back = lax.all_to_all(back_cols, "ctx", split_axis=1, concat_axis=0, tiled=True)
    conv_wide = conv_back.T.astype(jnp.float32)
    block_out = (query_rows * conv_wide).astype(jnp.bfloat16)
    grad_query = grad_out.astype(jnp.float32) * conv_wide
    back_rows = back_back.T
    back_after = from_behind(back_rows[: long_taps - 1], "ctx", -1)
    grad_gated = depthwise(
        jnp.concatenate([back_rows, back_after], 0).astype(jnp.float32), medium_filter
    )
    grad_medium_part = depthwise(gated_wide, back_rows.astype(jnp.float32))[::-1]
    streams = jnp.concatenate(
        [grad_query, grad_gated * value_rows, grad_gated * key_rows], 1
    ).astype(jnp.bfloat16)
    stream_after = from_behind(streams[: short_taps - 1], "ctx", -1)
    grad_three = depthwise(
        jnp.concatenate([streams, stream_after], 0).astype(jnp.float32), filter_bank
    )
    grad_normed = (
        grad_three[:, :channels]
        + grad_three[:, channels : 2 * channels]
        + grad_three[:, 2 * channels :]
    )
    short_lagged = depthwise(jnp.tile(normed_window, (1, 3)), streams.astype(jnp.float32))[::-1]
    grad_short_part = short_lagged.reshape(short_taps, 3, channels).transpose(1, 0, 2)
    grad_gain_part = jnp.sum(grad_normed * widened * inv_rms[:, None], axis=0)
    grad_gain, grad_short, grad_medium = lax.psum(
        (grad_gain_part, grad_short_part, grad_medium_part), "ctx"
    )
    scaled = grad_normed * norm_gain
    dot_sums = lax.psum(jnp.sum(scaled * widened, axis=1), "tp")
    cubed = inv_rms * inv_rms * inv_rms
    grad_tokens = (
        inv_rms[:, None] * scaled - widened * (cubed * dot_sums / total_chans)[:, None]
    ).astype(jnp.bfloat16)
    return (
        block_out,
        grad_tokens,
        grad_gain,
        grad_short,
        grad_medium,
        grad_skip,
        grad_residues,
        grad_decay,
    )


def solution(mesh):
    in_specs = (
        P("ctx", "tp"),
        P("tp"),
        P(None, None, "tp"),
        P(None, "tp"),
        P(("tp", "ctx"), None),
        P(("tp", "ctx"), None),
        P(("tp", "ctx")),
        P("ctx", "tp"),
    )
    out_specs = (
        P("ctx", "tp"),
        P("ctx", "tp"),
        P("tp"),
        P(None, None, "tp"),
        P(None, "tp"),
        P(("tp", "ctx")),
        P(("tp", "ctx"), None),
        P(("tp", "ctx"), None),
    )
    return jax.shard_map(
        per_device, mesh=mesh, in_specs=in_specs, out_specs=out_specs, check_vma=False
    )
```

profile of v0, /device:TPU:8, one launch (start us, length us, event | category | flops | bytes accessed | tf_op | source)
XLA Modules:
  0.0 485.4 jit_solution(17025651267544901190)
XLA Ops:
  8.3 9.9 %psum.35 = f32[128]{0:T(128)S(1)} all-reduce(f32[128]{0:T(128)S(1)} %fusion.71), channel_id=1, replica_groups=mesh['ctx'=64,'tp'=4] {'tp'}, use_global_device_ids=true, to_apply=%region_1.0 | all-reduce | flops 128 | bytes 1024 | tf_op jit(solution)/shard_map/psum | solution.py:149
  19.8 1.9 collective-permute-start
  23.8 2.6 convolution_negate_fusion
  26.5 2.6 fusion.196
  29.1 1.2 fusion.24
  30.4 2.2 convolution_subtract_fusion.4
  33.8 11.1 %rev.12 = f32[3,3072]{1,0:T(4,128)} reverse(f32[3,3072]{1,0:T(4,128)} %bitcast.329), dimensions={0} | reverse | bytes 73728 | tf_op jit(solution)/shard_map/rev | solution.py:155
  44.9 1.4 broadcast_in_dim.14
  46.4 4.7 rev.13
  51.9 2.0 tile.4
  53.8 4.0 tile.5
  57.9 2.8 pad
  60.6 4.1 reshape.797
  64.7 1.7 copy.135
  66.9 2.4 copy.136
  69.4 3.0 reshape.801
  72.4 1.6 slice_bitcast_fusion.1
  75.2 3.5 collective-permute-start.1
  78.7 2.2 convolution_add_fusion.4
  81.8 10.3 %all-to-all-start.2 = ((bf16[64,16,128]{2,1,0:T(8,128)(2,1)}), bf16[64,16,128]{2,1,0:T(8,128)(2,1)S(1)}, u32[]{:S(2)}, u32[]{:S(2)}) async-start(bf16[64,16,128]{2,1,0:T(8,128)(2,1)} %bitcast.56), calls=%async_computation.2 | async-start | bytes 524288 | tf_op jit(solution)/shard_map/all_to_all | solution.py:168
  93.2 5.8 %convolution_convert_fusion = bf16[1,128,1024]{2,0,1:T(2,128)(2,1)S(1)} fusion(bf16[1,255,1024]{2,1,0:T(8,128)(2,1)S(1)} %maximum_bitcast_fusion.1, f32[128,1,1024]{2,0,1:T(8,128)S(1)} %bitcast.326), kind=kOutput, calls=%fused_computation.39 | convolution fusion | flops 201457664 | bytes 1308672 | tf_op jit(solution)/shard_map/conv_general_dilated | solution.py:20
  100.1 4.0 all-to-all-done.2
  104.1 6.8 %all-to-all-start = ((bf16[64,16,128]{2,1,0:T(8,128)(2,1)}), bf16[64,16,128]{2,1,0:T(8,128)(2,1)S(1)}, u32[]{:S(2)}, u32[]{:S(2)}) async-start(bf16[64,16,128]{2,1,0:T(8,128)(2,1)} %bitcast.9), calls=%async_computation | async-start | bytes 524288 | tf_op jit(solution)/shard_map/all_to_all | solution.py:165
  112.4 1.2 fusion.18
  113.6 2.2 convolution_subtract_fusion.2
  115.8 1.2 fusion.22
  117.1 2.2 convolution_add_fusion.2
  119.3 3.2 all-to-all-done
  126.4 1.2 convolution_add_fusion.5
  128.6 2.0 multiply_add_fusion
  134.2 1.2 convolution_add_fusion
  136.8 4.4 multiply_reduce_fusion
  141.2 1.4 fusion.161
  149.2 7.7 %all-to-all-start.3 = ((bf16[16,64,128]{2,0,1:T(8,128)(2,1)}), bf16[16,64,128]{2,0,1:T(8,128)(2,1)}, u32[]{:S(2)}, u32[]{:S(2)}) async-start(bf16[16,64,128]{2,0,1:T(8,128)(2,1)} %copy.162), calls=%async_computation.3 | async-start | bytes 524288 | tf_op jit(solution)/shard_map/all_to_all | solution.py:172
  164.9 1.6 fusion.16
  168.7 9.8 %all-to-all-start.1 = ((bf16[16,64,128]{2,0,1:T(8,128)(2,1)}), bf16[16,64,128]{2,0,1:T(8,128)(2,1)S(1)}, u32[]{:S(2)}, u32[]{:S(2)}) async-start(bf16[16,64,128]{2,0,1:T(8,128)(2,1)} %copy.158), calls=%async_computation.1 | async-start | bytes 524288 | tf_op jit(solution)/shard_map/all_to_all | solution.py:167
  178.6 1.3 collective-permute-start.2
  179.9 1.3 copy.175
  181.3 7.8 %fusion.65 = f32[1,128,1024]{2,0,1:T(1,128)S(1)} fusion(bf16[128,1,1024]{2,1,0:T(2,128)(2,1)S(1)} %copy.175, bf16[1,255,1024]{2,1,0:T(8,128)(2,1)S(1)} %copy-done.15), kind=kOutput, calls=%fused_computation.106 | convolution fusion | flops 33554432 | bytes 1308672 | tf_op jit(solution)/shard_map/conv_general_dilated | solution.py:20
  189.1 2.6 rev.15
  194.2 6.0 %fusion.82 = f32[1,128,1024]{2,0,1:T(1,128)S(1)} fusion(bf16[1,255,1024]{2,0,1:T(2,128)(2,1)S(1)} %copy.164, f32[128,1,1024]{2,0,1:T(8,128)S(1)} %bitcast.325), kind=kOutput, calls=%fused_computation.137 | convolution fusion | flops 201326592 | bytes 1570816 | tf_op jit(solution)/shard_map/conv_general_dilated | solution.py:20
  201.4 1.4 collective-permute-start.3
  202.9 3.6 fusion.5
  209.6 1.4 reshape.808
  211.0 1.6 slice_bitcast_fusion
  212.9 10.2 %psum.36 = f32[128]{0:T(128)S(1)} all-reduce(f32[128]{0:T(128)S(1)} %get-tuple-element.41), channel_id=1, replica_groups=mesh['ctx'=64,'tp'=4] {'tp'}, use_global_device_ids=true, to_apply=%region_3.4 | all-reduce | flops 128 | bytes 1024 | tf_op jit(solution)/shard_map/psum | solution.py:201
  223.1 252.2 %all-reduce = (f32[1024]{0:T(1024)}, f32[3,3,1024]{2,1,0:T(4,128)}) all-reduce(f32[1024]{0:T(1024)S(1)} %get-tuple-element.40, f32[3,3,1024]{2,1,0:T(4,128)S(1)} %bitcast.327), channel_id=1, replica_groups=mesh['ctx'=64,'tp'=4] {'ctx'}, use_global_device_ids=true, to_apply=%region_5.6 | all-reduce | flops 10240 | bytes 81920 | tf_op jit(solution)/shard_map/psum | solution.py:197
  476.2 1.9 copy.229
  (264 shorter events, 46.3 us)
Async XLA Ops:
  18.1 5.2 %copy-start.89 = (f32[128]{0:T(128)}, f32[128]{0:T(128)S(1)}, u32[]{:S(2)}) copy-start(f32[128]{0:T(128)S(1)} %psum.35) | copy-start | bytes 1540
  18.1 1.7 copy-start.22
  19.8 31.3 %collective-permute-start = (bf16[2,1024]{1,0:T(2,128)(2,1)}, bf16[2,1024]{1,0:T(2,128)(2,1)}, u32[]{:S(2)}, u32[]{:S(2)}) collective-permute-start(bf16[2,1024]{1,0:T(2,128)(2,1)} %slice.252), channel_id=1, source_target_pairs={{0,4},{4,8},{8,12},{12,16},{16,20},{20,24},{24,28},{28,32},{32,36}... | collective-permute-start | bytes 12296 | tf_op jit(solution)/shard_map/ppermute | solution.py:16
  23.3 3.1 copy-start.20
  23.6 2.8 copy-start.25
  23.6 2.8 copy-start.27
  23.7 2.8 copy-start.29
  23.7 2.8 copy-start.31
  23.7 2.8 copy-start.33
  23.7 2.8 copy-start.35
  23.7 2.8 copy-start.37
  23.7 2.8 copy-start.39
  23.7 2.8 copy-start.41
  23.7 2.8 copy-start.43
  23.7 2.8 copy-start.45
  23.7 2.8 copy-start.47
  23.8 2.8 copy-start.49
  23.8 2.8 copy-start.51
  23.8 2.8 copy-start.53
  23.8 2.8 copy-start.55
  64.7 1.8 copy-start.19
  64.7 1.8 copy-start.91
  72.4 1.6 copy-start.11
  74.0 6.9 %copy-start = (f32[128,3072]{1,0:T(8,128)}, f32[128,3072]{1,0:T(8,128)S(1)}, u32[]{:S(2)}) copy-start(f32[128,3072]{1,0:T(8,128)S(1)} %slice_bitcast_fusion.1) | copy-start | bytes 4718596
  74.2 6.7 %copy-start.10 = (bf16[128,1024]{1,0:T(8,128)(2,1)}, bf16[128,1024]{1,0:T(8,128)(2,1)S(1)}, u32[]{:S(2)}) copy-start(bf16[128,1024]{1,0:T(8,128)(2,1)S(1)} %get-tuple-element.121) | copy-start | bytes 786436
  75.2 16.9 %collective-permute-start.1 = (bf16[127,1024]{1,0:T(8,128)(2,1)}, bf16[127,1024]{1,0:T(8,128)(2,1)}, u32[]{:S(2)}, u32[]{:S(2)}) collective-permute-start(bf16[127,1024]{1,0:T(8,128)(2,1)} %slice.258), channel_id=1, source_target_pairs={{0,4},{4,8},{8,12},{12,16},{16,20},{20,24},{24,28},{28,32},{32,36}... | collective-permute-start | bytes 780296 | tf_op jit(solution)/shard_map/ppermute | solution.py:16
  80.9 12.3 %copy-start.16 = (f32[128,1024]{1,0:T(8,128)S(1)}, f32[128,1024]{1,0:T(8,128)}, u32[]{:S(2)}) copy-start(f32[128,1024]{1,0:T(8,128)} %rev.13) | copy-start | bytes 1572868
  81.8 22.3 %all-to-all-start.2 = ((bf16[64,16,128]{2,1,0:T(8,128)(2,1)}), bf16[64,16,128]{2,1,0:T(8,128)(2,1)S(1)}, u32[]{:S(2)}, u32[]{:S(2)}) async-start(bf16[64,16,128]{2,1,0:T(8,128)(2,1)} %bitcast.56), calls=%async_computation.2 | async-start | bytes 524288 | tf_op jit(solution)/shard_map/all_to_all | solution.py:168
  93.2 5.8 %copy-start.14 = (bf16[1,255,1024]{2,1,0:T(8,128)(2,1)}, bf16[1,255,1024]{2,1,0:T(8,128)(2,1)S(1)}, u32[]{:S(2)}) copy-start(bf16[1,255,1024]{2,1,0:T(8,128)(2,1)S(1)} %maximum_bitcast_fusion.1) | copy-start | bytes 1566724
  104.1 18.3 %all-to-all-start = ((bf16[64,16,128]{2,1,0:T(8,128)(2,1)}), bf16[64,16,128]{2,1,0:T(8,128)(2,1)S(1)}, u32[]{:S(2)}, u32[]{:S(2)}) async-start(bf16[64,16,128]{2,1,0:T(8,128)(2,1)} %bitcast.9), calls=%async_computation | async-start | bytes 524288 | tf_op jit(solution)/shard_map/all_to_all | solution.py:165
  122.4 2.8 copy-start.3
  126.4 1.5 copy-start.6
  126.4 1.8 copy-start.7
  126.4 2.1 copy-start.8
  149.2 19.5 %all-to-all-start.3 = ((bf16[16,64,128]{2,0,1:T(8,128)(2,1)}), bf16[16,64,128]{2,0,1:T(8,128)(2,1)}, u32[]{:S(2)}, u32[]{:S(2)}) async-start(bf16[16,64,128]{2,0,1:T(8,128)(2,1)} %copy.162), calls=%async_computation.3 | async-start | bytes 524288 | tf_op jit(solution)/shard_map/all_to_all | solution.py:172
  162.1 2.7 copy-start.4
  166.5 14.8 %copy-start.15 = (bf16[1,255,1024]{2,1,0:T(8,128)(2,1)S(1)}, bf16[1,255,1024]{2,1,0:T(8,128)(2,1)}, u32[]{:S(2)}) copy-start(bf16[1,255,1024]{2,1,0:T(8,128)(2,1)} %copy-done.14) | copy-start | bytes 1566724
  168.7 23.1 %all-to-all-start.1 = ((bf16[16,64,128]{2,0,1:T(8,128)(2,1)}), bf16[16,64,128]{2,0,1:T(8,128)(2,1)S(1)}, u32[]{:S(2)}, u32[]{:S(2)}) async-start(bf16[16,64,128]{2,0,1:T(8,128)(2,1)} %copy.158), calls=%async_computation.1 | async-start | bytes 524288 | tf_op jit(solution)/shard_map/all_to_all | solution.py:167
  178.6 297.6 %all-reduce.3.cloned.1.call-start = ((), (), s32[]{:S(2)}) async-start(), calls=%async_computation.4 | async-start | bytes 1048576 | tf_op jit(solution)/shard_map/psum | solution.py:197
  178.6 13.4 %collective-permute-start.2 = (bf16[127,1024]{0,1:T(8,128)(2,1)}, bf16[127,1024]{0,1:T(8,128)(2,1)S(1)}, u32[]{:S(2)}, u32[]{:S(2)}) collective-permute-start(bf16[127,1024]{0,1:T(8,128)(2,1)} %bitcast.319), channel_id=1, source_target_pairs={{4,0},{8,4},{12,8},{16,12},{20,16},{24,20},{28,24},{32,28},{36,32}... | collective-permute-start | bytes 780296 | tf_op jit(solution)/shard_map/ppermute | solution.py:16
  191.8 2.4 copy-start.13
  194.2 6.0 %copy-start.1 = (f32[128,3072]{1,0:T(8,128)S(1)}, f32[128,3072]{1,0:T(8,128)}, u32[]{:S(2)}) copy-start(f32[128,3072]{1,0:T(8,128)} %copy-done) | copy-start | bytes 4718596
  194.2 6.0 %copy-start.12 = (bf16[128,1024]{1,0:T(8,128)(2,1)S(1)}, bf16[128,1024]{1,0:T(8,128)(2,1)}, u32[]{:S(2)}) copy-start(bf16[128,1024]{1,0:T(8,128)(2,1)} %param.15) | copy-start | bytes 786436
  201.4 5.8 %collective-permute-start.3 = (bf16[2,3072]{1,0:T(2,128)(2,1)S(1)}, bf16[2,3072]{1,0:T(2,128)(2,1)S(1)}, u32[]{:S(2)}, u32[]{:S(2)}) collective-permute-start(bf16[2,3072]{1,0:T(2,128)(2,1)S(1)} %pad_maximum_fusion.1), channel_id=1, source_target_pairs={{4,0},{8,4},{12,8},{16,12},{20,16},{24,20},{28,24},{32,28},{36,32}... | collective-permute-start | bytes 36872 | tf_op jit(solution)/shard_map/ppermute | solution.py:16
  211.0 1.6 copy-start.9
  211.0 1.6 copy-start.18
  211.0 1.6 copy-start.23
  212.6 10.5 %copy-start.90 = (f32[128]{0:T(128)S(1)}, f32[128]{0:T(128)}, u32[]{:S(2)}) copy-start(f32[128]{0:T(128)} %copy-done.89) | copy-start | bytes 1540
  (54 other events, 66.3 us)
Sparse Core Ops, SparseCore 0:
  191.9 185.3 all-reduce.2
where the time goes:
time: 494 us; the launch traced here: 485 us
  blocking collectives  272 us (55%)
  matrix products  76.2 us (15%)
  local copies, waits for them, and re-layouts  61.2 us (12%)
  starting transfers between devices  42.8 us (9%)
  between operations  16.4 us (3%)
  other arithmetic  8.69 us (2%)
  waiting for transfers between devices  7.73 us (2%)
    psum x1, blocking collectives, per_device(): lax.psum((grad_gain_part, grad_short_part, grad_medium_part), 'ctx')  252 us
    dot_general x36, matrix products, contract(): jnp.einsum(pattern, operand, matrix, precision=HIGHEST, preferred_element...  52.3 us
    conv_general_dilated x6, matrix products, depthwise(): lax.conv_general_dilated(extended[None], weights[:, None, :], (1,), 'VALI...  23.9 us
    conv_general_dilated x10, local copies, waits for them, and re-layouts, depthwise(): lax.conv_general_dilated(extended[None], weights[:, None, :], (1,), 'VALI...  14.6 us
    rev x1, local copies, waits for them, and re-layouts, per_device(): mixed_rows = depthwise(jnp.tile(normed_window, (1, 3)), filter_bank[::-1])  11.1 us
    all_to_all x1, starting transfers between devices, per_device(): lax.all_to_all(grad_gate.T, 'ctx', split_axis=0, concat_axis=1, tiled=True)  10.3 us
    psum x1, blocking collectives, per_device(): dot_sums = lax.psum(jnp.sum(scaled * widened, axis=1), 'tp')  10.2 us
  transfers between devices with their start and end apart: 9, of which 3 were waited for; matrix products, arithmetic and copies ran while one was open for 19% of the time, Pallas kernels for 0%

commit v1 on v0

v1 whole, which is shorter than its diff:
```python
import functools
import math

import jax
import jax.numpy as jnp
import ml_dtypes
import numpy as np
from jax import lax
from jax.experimental import pallas as pl
from jax.experimental.pallas import tpu as pltpu
from jax.sharding import PartitionSpec as P

EPSILON = 1e-06
HIGHEST = lax.Precision.HIGHEST
MESH = pl.DeviceIdType.MESH
TOK = 128
MODES = 16
LANES = 128
f32 = jnp.float32
bf16 = jnp.bfloat16
VMEM_SPEC = pl.BlockSpec(memory_space=pltpu.VMEM)


def transform_tables():
    freq = 2 * np.arange(TOK)[:, None] + 1
    angle = np.pi / 256.0 * ((freq * np.arange(256)[None, :]) % 512)
    table = np.concatenate([np.cos(angle), -np.sin(angle)], 0)

    def two(matrix):
        high = matrix.astype(ml_dtypes.bfloat16)
        return high, (matrix - high.astype(np.float64)).astype(ml_dtypes.bfloat16)

    high, low = two(table)
    near, far = slice(0, TOK), slice(TOK, 256)
    inv_near, inv_near_low = two(table[:, near].T / 128.0)
    inv_far, inv_far_low = two(table[:, far].T / 128.0)
    cat = lambda *parts: np.concatenate(parts, 1)
    return {
        "whole2": cat(high, low),
        "near2": cat(high[:, near], low[:, near]),
        "far2": cat(high[:, far], low[:, far]),
        "near3": cat(high[:, near], high[:, near], low[:, near]),
        "inv_near3": cat(inv_near, inv_near, inv_near_low),
        "inv_far3": cat(inv_far, inv_far, inv_far_low),
    }


def lane_orders():
    order = np.zeros((2, 64, LANES), np.float32)
    for half in range(2):
        for row in range(64):
            order[half, row, 16 * (row // 8) + 8 * half + row % 8] = 1.0
    return order


def dot2(table, data):
    return jnp.dot(table, jnp.concatenate([data, data], 0), preferred_element_type=f32)


def dot3(table, data):
    high = data.astype(bf16)
    low = (data - high.astype(f32)).astype(bf16)
    return jnp.dot(table, jnp.concatenate([high, low, high], 0), preferred_element_type=f32)


def halves(spectrum):
    return spectrum[:TOK], spectrum[TOK:]


def product(first, second):
    (a, b), (c, d) = halves(first), halves(second)
    return jnp.concatenate([a * c - b * d, a * d + b * c], 0)


def product_conj(first, second):
    (a, b), (c, d) = halves(first), halves(second)
    return jnp.concatenate([a * c + b * d, b * c - a * d], 0)


def eye(size):
    return (lax.broadcasted_iota(jnp.int32, (size, size), 0) == lax.broadcasted_iota(jnp.int32, (size, size), 1)).astype(f32)


def to_column(row):
    return jnp.sum(eye(row.shape[1]) * row, axis=1, keepdims=True)


def to_row(column):
    return jnp.sum(eye(column.shape[0]) * column, axis=0, keepdims=True)


def place(row, step, part, lane_blocks):
    if lane_blocks == 1:
        return row // 2, row % 2
    return row * (lane_blocks // 2) + step, part


def greet(barrier, count, axis, skip=0):
    me = lax.axis_index(axis)

    def body(d, carry):
        pl.semaphore_signal(barrier, inc=1, device_id={axis: lax.rem(me + d, count)}, device_id_type=MESH)
        return carry

    lax.fori_loop(1, count, body, 0)


def send(src, dst, send_sem, recv_sem, **where):
    return pltpu.make_async_remote_copy(src, dst, send_sem, recv_sem, device_id=where, device_id_type=MESH)


def each(first, last, work):
    def body(d, carry):
        work(d)
        return carry

    lax.fori_loop(first, last, body, 0)


def entry_kernel(n, n_tp, total, tok_ref, res_ref, rate_ref, skip_ref,
                 inv_ref, prev_ref, prev2_ref, par_ref,
                 msg, sums, sums_in, inv_own, psend, precv, tsend, trecv, ssend, srecv, isend, irecv):
    me = lax.axis_index("ctx")
    tp = lax.axis_index("tp")
    barrier = pltpu.get_barrier_semaphore()
    greet(barrier, n, "ctx")
    greet(barrier, n_tp, "tp")
    length = n * TOK
    msg[...] = jnp.zeros(msg.shape, f32)
    msg[:, 0:16] = res_ref[0:8, :]
    msg[:, 16:32] = res_ref[8:16, :]
    msg[:, 32:48] = rate_ref[0:8, :] / length
    msg[:, 48:64] = rate_ref[8:16, :] / length
    skip_col = to_column(skip_ref[...])
    msg[:, 64:65] = skip_col[0:8]
    msg[:, 65:66] = skip_col[8:16]
    wide = tok_ref[...].astype(f32)
    sums[...] = jnp.broadcast_to(to_row(jnp.sum(wide * wide, axis=1, keepdims=True)), sums.shape)
    pl.semaphore_wait(barrier, n - 1 + n_tp - 1)

    def sum_copy(d):
        return send(sums, sums_in.at[d], ssend.at[d], srecv.at[d], tp=lax.rem(tp + d, n_tp))

    def par_copy(d):
        return send(msg, par_ref.at[me], psend.at[d], precv.at[d], ctx=lax.rem(me + d, n))

    one = lax.rem(me + 1, n)
    two = lax.rem(me + 2, n)
    tok_copy = send(tok_ref, prev_ref, tsend.at[0], trecv.at[0], ctx=one)
    tail_copy = send(tok_ref.at[pl.ds(TOK - 16, 16)], prev2_ref, tsend.at[1], trecv.at[1], ctx=two)
    for d in range(1, n_tp):
        sum_copy(d).start()
    tail_copy.start()
    tok_copy.start()
    each(1, n, lambda d: par_copy(d).start())
    par_ref[me] = msg[...]
    squares = sums[...]
    for d in range(1, n_tp):
        sum_copy(d).wait_recv()
        squares = squares + sums_in[d]
    inv_own[...] = lax.rsqrt(squares / total + EPSILON)
    inv_copies = [
        send(inv_own, inv_ref.at[1], isend.at[0], irecv.at[0], ctx=one),
        send(inv_own, inv_ref.at[2], isend.at[1], irecv.at[1], ctx=two),
    ]
    for copy in inv_copies:
        copy.start()
    inv_ref[0] = inv_own[...]
    for copy in inv_copies + [tok_copy, tail_copy]:
        copy.wait()
    for d in range(1, n_tp):
        sum_copy(d).wait_send()
    each(1, n, lambda d: par_copy(d).wait())


def entry(tokens, residues, decay_rate, skip_gain, total):
    n, n_tp = lax.axis_size("ctx"), lax.axis_size("tp")
    channels = tokens.shape[1]
    dma = pltpu.SemaphoreType.DMA
    return pl.pallas_call(
        functools.partial(entry_kernel, n, n_tp, total),
        out_shape=(
            jax.ShapeDtypeStruct((3, 8, TOK), f32),
            jax.ShapeDtypeStruct((TOK, channels), bf16),
            jax.ShapeDtypeStruct((16, channels), bf16),
            jax.ShapeDtypeStruct((n, 8, LANES), f32),
        ),
        in_specs=[VMEM_SPEC] * 4,
        out_specs=[VMEM_SPEC] * 4,
        scratch_shapes=[
            pltpu.VMEM((8, LANES), f32), pltpu.VMEM((8, TOK), f32), pltpu.VMEM((n_tp, 8, TOK), f32), pltpu.VMEM((8, TOK), f32),
            dma((n,)), dma((n,)), dma((2,)), dma((2,)), dma((n_tp,)), dma((n_tp,)), dma((2,)), dma((2,)),
        ],
        compiler_params=pltpu.CompilerParams(collective_id=1, has_side_effects=True),
        name="entry",
    )(tokens, residues, decay_rate, skip_gain.reshape(1, -1))


def powers(rate_row, exponents):
    return jnp.exp(-rate_row * exponents)


def sublanes():
    return lax.broadcasted_iota(jnp.int32, (8, LANES), 0).astype(f32)


def horner(blocks, eighth):
    total = blocks[-1]
    moment = jnp.zeros_like(total)
    for block in blocks[-2::-1]:
        shifted = eighth * total
        moment = eighth * moment + shifted
        total = shifted + block
    return total, moment


def down(values):
    return jnp.sum(values, axis=0, keepdims=True)


def forward_kernel(n, lane_blocks, inv_ref, tok_ref, prev_ref, prev2_ref, gain_ref, sf_ref, mf_ref, par_ref, gout_ref,
                   order_ref, whole2, near2, near3, inv_near3, inv_far3,
                   q_ref, k_ref, v_ref, normed_ref, gspec_ref, mspec_ref, conv_ref, back_ref, gskip_ref,
                   sr_ref, aux_ref, rows_ref, ext, kern, sig, grd, kgr):
    step = pl.program_id(0)
    width = tok_ref.shape[1]
    me = lax.axis_index("ctx")
    gain = gain_ref[...]

    def normed_of(values, inv_row, live):
        scale = to_column(inv_row)[TOK - values.shape[0]:]
        rounded = (values.astype(f32) * scale * gain).astype(bf16).astype(f32)
        return jnp.where(live, rounded, 0.0)

    ext[0:16] = normed_of(prev2_ref[...], inv_ref[2, 0:1], me >= 2)
    ext[16:144] = normed_of(prev_ref[...], inv_ref[1, 0:1], me >= 1)
    ext[144:272] = normed_of(tok_ref[...], inv_ref[0, 0:1], me >= 0)
    normed_ref[...] = ext[136:272]

    def stream(s, first, count):
        total = sf_ref[3 * s:3 * s + 1] * ext[first:first + count]
        for j in range(1, 3):
            total = total + sf_ref[3 * s + j:3 * s + j + 1] * ext[first - j:first - j + count]
        return total

    query = stream(0, 144, TOK)
    q_ref[...] = query
    keys = stream(1, 16, 256)
    values = stream(2, 16, 256)
    k_ref[...] = keys[TOK:]
    v_ref[...] = values[TOK:]
    gated = (keys * values).astype(bf16)
    gspec = dot2(whole2[...], gated)
    mspec = dot3(near3[...], mf_ref[...])
    gspec_ref[...] = gspec
    mspec_ref[...] = mspec
    signal = dot3(inv_far3[...], product(gspec, mspec)).astype(bf16)
    grad_gate = (gout_ref[...].astype(f32) * query).astype(bf16)
    sig[...] = signal.astype(f32)
    grd[...] = grad_gate.astype(f32)
    gskip_ref[...] = down(sig[...] * grd[...])

    r = sublanes()
    tables = []
    for part in range(width // LANES):
        lanes = slice(part * LANES, (part + 1) * LANES)
        packed = par_ref[8 * part:8 * part + 8].reshape(64, LANES).T
        even = jnp.dot(packed, order_ref[0], precision=HIGHEST, preferred_element_type=f32)
        odd = jnp.dot(packed, order_ref[1], precision=HIGHEST, preferred_element_type=f32)
        res = even[0:16] + odd[16:32]
        rate = even[32:48] + odd[48:64]
        skip = even[64:65] + odd[65:66]
        weight = res * jnp.sqrt(rate)
        eighths = []
        running = []
        for m in range(MODES):
            eighths.append(jnp.broadcast_to(jnp.exp(-8.0 * rate[m:m + 1]), (8, LANES)))
            running.append(weight[m:m + 1] * powers(rate[m:m + 1], r))
            piece, row = place(m, step, part, lane_blocks)
            rows_ref[piece, pl.ds(row, 1)] = res[m:m + 1]
            rows_ref[piece, pl.ds(2 + row, 1)] = rate[m:m + 1]
            rows_ref[piece, pl.ds(4 + row, 1)] = jnp.exp(-float(TOK) * rate[m:m + 1])
        for block in range(16):
            total = running[0]
            for m in range(1, MODES):
                total = total + running[m]
            if block == 0:
                total = total + jnp.where(r == 0.0, skip, 0.0)
            kern[8 * block:8 * block + 8, lanes] = total
            running = [value * eighth for value, eighth in zip(running, eighths)]
        tables.append((rate, eighths))
    kspec = dot3(near3[...], kern[...])
    uspec = dot2(near2[...], signal)
    cspec = dot2(near2[...], grad_gate)
    conv_ref[...] = dot3(inv_near3[...], product(kspec, uspec))
    back_ref[...] = dot3(inv_near3[...], product_conj(cspec, kspec))
    kgr[...] = dot3(inv_near3[...], product_conj(cspec, uspec))
    for part in range(width // LANES):
        lanes = slice(part * LANES, (part + 1) * LANES)
        rate, eighths = tables[part]
        for m in range(MODES):
            piece, row = place(m, step, part, lane_blocks)
            rising = powers(rate[m:m + 1], r)
            falling = powers(rate[m:m + 1], 7.0 - r)
            load = lambda ref: [ref[8 * b:8 * b + 8, lanes] for b in range(16)]
            total, moment = horner(load(sig)[::-1], eighths[m])
            sr_ref[piece, pl.ds(row, 1)] = down(falling * total)
            aux_ref[piece, pl.ds(row, 1)] = down(falling * (8.0 * moment + (7.0 - r) * total))
            total, moment = horner(load(grd), eighths[m])
            sr_ref[piece, pl.ds(2 + row, 1)] = down(rising * total)
            aux_ref[piece, pl.ds(2 + row, 1)] = down(rising * (8.0 * moment + r * total))
            total, moment = horner(load(kgr), eighths[m])
            aux_ref[piece, pl.ds(4 + row, 1)] = down(rising * total)
            aux_ref[piece, pl.ds(6 + row, 1)] = down(rising * (8.0 * moment + r * total))


def split_lanes(rows, width):
    return pl.BlockSpec((rows, width), lambda i: (0, i))


def whole(*shape):
    return pl.BlockSpec(shape, lambda i: (0,) * len(shape))


def block_width(channels):
    return min(256, channels)


def forward(inv, tokens, prev, prev2, gain, short, medium, par, grad_out, tables, order):
    channels = tokens.shape[1]
    width = block_width(channels)
    n = par.shape[0]
    lane_blocks = channels // LANES
    lanes = lambda rows: split_lanes(rows, width)
    names = ("whole2", "near2", "near3", "inv_near3", "inv_far3")
    mats = [tables[name] for name in names]
    wide = lambda rows: jax.ShapeDtypeStruct((rows, channels), f32)
    return pl.pallas_call(
        functools.partial(forward_kernel, n, lane_blocks),
        grid=(channels // width,),
        out_shape=(wide(TOK), wide(TOK), wide(TOK), wide(136), wide(256), wide(256), wide(TOK), wide(TOK), wide(1),
                   jax.ShapeDtypeStruct((n, 4, LANES), f32), jax.ShapeDtypeStruct((n, 8, LANES), f32), jax.ShapeDtypeStruct((n, 8, LANES), f32)),
        in_specs=[whole(3, 8, TOK), lanes(TOK), lanes(TOK), lanes(16), lanes(1), lanes(9), lanes(TOK),
                  pl.BlockSpec((8 * width // LANES, 8, LANES), lambda i: (i, 0, 0)), lanes(TOK), whole(2, 64, LANES)]
        + [whole(*mat.shape) for mat in mats],
        out_specs=[lanes(TOK), lanes(TOK), lanes(TOK), lanes(136), lanes(256), lanes(256), lanes(TOK), lanes(TOK), lanes(1),
                   whole(n, 4, LANES), whole(n, 8, LANES), whole(n, 8, LANES)],
        scratch_shapes=[pltpu.VMEM((272, width), f32)] + [pltpu.VMEM((TOK, width), f32)] * 4,
        name="forward",
    )(inv, tokens, prev, prev2, gain, short, medium, par, grad_out, order, *mats)


def states_kernel(n, sr_ref, rows_ref, hq_ref, inbox, outbox, send1, recv1, send2, recv2):
    me = lax.axis_index("ctx")
    barrier = pltpu.get_barrier_semaphore()
    greet(barrier, n, "ctx")
    pl.semaphore_wait(barrier, n - 1)

    def out_copy(d):
        peer = lax.rem(me + d, n)
        return send(sr_ref.at[peer], inbox.at[me], send1.at[d], recv1.at[d], ctx=peer)

    def back_copy(d):
        peer = lax.rem(me + d, n)
        return send(outbox.at[peer], hq_ref.at[me], send2.at[d], recv2.at[d], ctx=peer)

    each(1, n, lambda d: out_copy(d).start())
    inbox[me] = sr_ref[me]
    decay = rows_ref[me][4:6]
    each(1, n, lambda d: out_copy(d).wait())

    def scan(i, carry):
        ahead, behind = carry
        j = n - 1 - i
        outbox[i, 0:2] = ahead
        outbox[j, 2:4] = behind
        return decay * ahead + inbox[i][0:2], decay * behind + inbox[j][2:4]

    zero = jnp.zeros((2, LANES), f32)
    lax.fori_loop(0, n, scan, (zero, zero))
    each(1, n, lambda d: back_copy(d).start())
    hq_ref[me] = outbox[me]
    each(1, n, lambda d: back_copy(d).wait())


def states(sr, rows):
    n = sr.shape[0]
    dma = pltpu.SemaphoreType.DMA
    return pl.pallas_call(
        functools.partial(states_kernel, n),
        out_shape=jax.ShapeDtypeStruct(sr.shape, f32),
        in_specs=[VMEM_SPEC] * 2,
        out_specs=VMEM_SPEC,
        scratch_shapes=[pltpu.VMEM(sr.shape, f32), pltpu.VMEM(sr.shape, f32)] + [dma((n,))] * 4,
        compiler_params=pltpu.CompilerParams(collective_id=2, has_side_effects=True),
        name="states",
    )(sr, rows)


def middle_kernel(lane_blocks, hq_ref, sr_ref, aux_ref, rows_ref, conv_ref, backl_ref, q_ref, gout_ref, gspec_ref,
                  near2, inv_near3, out_ref, back_ref, stream_ref, medium_ref, bspec_ref, fs_ref, ahead_scr, behind_scr):
    step = pl.program_id(0)
    width = q_ref.shape[1]
    r = sublanes()
    for part in range(width // LANES):
        lanes = slice(part * LANES, (part + 1) * LANES)
        eighths, ahead, behind = [], [], []
        for m in range(MODES):
            piece, row = place(m, step, part, lane_blocks)
            take = lambda ref, at: ref[piece, pl.ds(at + row, 1)]
            res, rate, chunk = take(rows_ref, 0), take(rows_ref, 2), take(rows_ref, 4)
            state, future = take(hq_ref, 0), take(hq_ref, 2)
            weight = res * jnp.sqrt(rate)
            single = jnp.exp(-rate)
            near = take(sr_ref, 2)
            fs_ref[piece, pl.ds(row, 1)] = take(aux_ref, 4) + single * near * state
            fs_ref[piece, pl.ds(2 + row, 1)] = take(aux_ref, 6) + single * (
                (near + take(aux_ref, 2)) * state + take(aux_ref, 0) * future + float(TOK) * chunk * state * future)
            eighths.append(jnp.broadcast_to(jnp.exp(-8.0 * rate), (8, LANES)))
            ahead.append(weight * state * powers(rate, r + 1.0))
            behind.append(weight * future * powers(rate, 8.0 - r))
        for block in range(16):
            other = 15 - block
            ahead_sum, behind_sum = ahead[0], behind[0]
            for m in range(1, MODES):
                ahead_sum = ahead_sum + ahead[m]
                behind_sum = behind_sum + behind[m]
            ahead_scr[8 * block:8 * block + 8, lanes] = ahead_sum
            behind_scr[8 * other:8 * other + 8, lanes] = behind_sum
            ahead = [value * eighth for value, eighth in zip(ahead, eighths)]
            behind = [value * eighth for value, eighth in zip(behind, eighths)]
    conv = (conv_ref[...] + ahead_scr[...]).astype(bf16).astype(f32)
    back = (backl_ref[...] + behind_scr[...]).astype(bf16)
    out_ref[...] = (q_ref[...] * conv).astype(bf16)
    stream_ref[...] = (gout_ref[...].astype(f32) * conv).astype(bf16)
    back_ref[...] = back
    bspec = dot2(near2[...], back)
    bspec_ref[...] = bspec
    sign = (1 - 2 * (lax.broadcasted_iota(jnp.int32, (TOK, width), 0) % 2)).astype(f32)
    real, imag = halves(bspec)
    late = jnp.concatenate([sign * imag, -sign * real], 0)
    medium_ref[...] = dot3(inv_near3[...], product_conj(late, gspec_ref[...])).astype(bf16)


def middle(hq, sr, aux, rows, conv, backl, query, grad_out, gspec, tables):
    channels = query.shape[1]
    width = block_width(channels)
    n = sr.shape[0]
    lanes = lambda count: split_lanes(count, width)
    mats = [tables[name] for name in ("near2", "inv_near3")]
    made = lambda count, kind: jax.ShapeDtypeStruct((count, channels), kind)
    return pl.pallas_call(
        functools.partial(middle_kernel, channels // LANES),
        grid=(channels // width,),
        out_shape=(made(TOK, bf16), made(TOK, bf16), made(TOK, bf16), made(TOK, bf16), made(256, f32), jax.ShapeDtypeStruct((n, 4, LANES), f32)),
        in_specs=[whole(n, 4, LANES), whole(n, 4, LANES), whole(n, 8, LANES), whole(n, 8, LANES), lanes(TOK), lanes(TOK), lanes(TOK), lanes(TOK), lanes(256)]
        + [whole(*mat.shape) for mat in mats],
        out_specs=[lanes(TOK)] * 4 + [lanes(256), whole(n, 4, LANES)],
        scratch_shapes=[pltpu.VMEM((TOK, width), f32)] * 2,
        name="middle",
    )(hq, sr, aux, rows, conv, backl, query, grad_out, gspec, *mats)


def tile_of(index, lane_blocks):
    rows = pl.multiple_of((index // lane_blocks) * 16, 16)
    lanes = pl.multiple_of((index % lane_blocks) * LANES, LANES)
    return (pl.ds(rows, 16), pl.ds(lanes, LANES))


def reduce_kernel(n, back_ref, medium_ref, fs_ref, next_ref, tile_ref, fsum_ref, tiles_in, fs_in, bsend, brecv, tsend, trecv, fsend, frecv):
    me = lax.axis_index("ctx")
    lane_blocks = medium_ref.shape[1] // LANES
    barrier = pltpu.get_barrier_semaphore()
    greet(barrier, n, "ctx")
    pl.semaphore_wait(barrier, n - 1)
    halo = send(back_ref, next_ref, bsend, brecv, ctx=lax.rem(me + n - 1, n))
    halo.start()

    def tile_copy(d):
        peer = lax.rem(me + d, n)
        return send(medium_ref.at[tile_of(peer, lane_blocks)], tiles_in.at[d], tsend.at[d], trecv.at[d], ctx=peer)

    def fs_copy(d):
        peer = lax.rem(me + d, n)
        return send(fs_ref.at[peer], fs_in.at[d], fsend.at[d], frecv.at[d], ctx=peer)

    def start(d):
        tile_copy(d).start()
        fs_copy(d).start()

    each(1, n, start)

    def add(d, totals):
        tile_copy(d).wait()
        fs_copy(d).wait()
        return totals[0] + tiles_in[d].astype(f32), totals[1] + fs_in[d]

    tile, sums = lax.fori_loop(1, n, add, (medium_ref[tile_of(me, lane_blocks)].astype(f32), fs_ref[me]))
    tile_ref[...] = tile.astype(bf16)
    fsum_ref[...] = sums
    halo.wait()


def reduce_medium(back, medium, fs):
    n = fs.shape[0]
    dma = pltpu.SemaphoreType.DMA
    return pl.pallas_call(
        functools.partial(reduce_kernel, n),
        out_shape=(jax.ShapeDtypeStruct(back.shape, bf16), jax.ShapeDtypeStruct((16, LANES), bf16), jax.ShapeDtypeStruct((4, LANES), f32)),
        in_specs=[VMEM_SPEC] * 3,
        out_specs=[VMEM_SPEC] * 3,
        scratch_shapes=[pltpu.VMEM((n, 16, LANES), bf16), pltpu.VMEM((n, 4, LANES), f32), dma, dma] + [dma((n,))] * 4,
        compiler_params=pltpu.CompilerParams(collective_id=3, has_side_effects=True),
        name="reduce_medium",
    )(back, medium, fs)


def backward_kernel(n, lane_blocks, inv_ref, next_ref, bspec_ref, mspec_ref, q_stream, k_ref, v_ref, normed_ref, tok_ref, prev_ref,
                    gain_ref, sf_ref, gskip_ref, far2, inv_near3, gn_ref, tail_ref, small_ref, dot_ref, pad0, pad1, pad2):
    step = pl.program_id(0)
    width = tok_ref.shape[1]
    me = lax.axis_index("ctx")
    later = jnp.where(me < n - 1, next_ref[...].astype(f32), 0.0).astype(bf16)
    spec = bspec_ref[...] + dot2(far2[...], later)
    grad_gated = dot3(inv_near3[...], product_conj(spec, mspec_ref[...]))
    streams = [
        q_stream[...].astype(f32),
        (grad_gated * v_ref[...]).astype(bf16).astype(f32),
        (grad_gated * k_ref[...]).astype(bf16).astype(f32),
    ]
    total = jnp.zeros((136, width), f32)
    rows = []
    for s, pad in enumerate((pad0, pad1, pad2)):
        pad[0:8] = jnp.zeros((8, width), f32)
        pad[8:136] = streams[s]
        pad[136:144] = jnp.zeros((8, width), f32)
        for j in range(3):
            total = total + sf_ref[3 * s + j:3 * s + j + 1] * pad[j:j + 136]
            rows.append(down(streams[s] * normed_ref[8 - j:136 - j]))
    tail = jnp.where(me >= 1, total[0:8], 0.0)
    grad_normed = total[8:136]
    gn_ref[...] = grad_normed
    tail_ref[...] = tail
    wide = tok_ref[...].astype(f32)
    inv = to_column(inv_ref[0, 0:1])
    before = to_column(inv_ref[1, 0:1])[TOK - 8:]
    rows.append(down(grad_normed * wide * inv) + down(tail * prev_ref[TOK - 16:TOK].astype(f32)[8:16] * before))
    rows.append(gskip_ref[...])
    scaled = grad_normed * gain_ref[...] * wide

    @pl.when(step == 0)
    def _():
        dot_ref[...] = jnp.zeros(dot_ref.shape, f32)
        small_ref[...] = jnp.zeros(small_ref.shape, f32)

    dots = dot_ref[...]
    for part in range(width // LANES):
        lanes = slice(part * LANES, (part + 1) * LANES)
        dots = dots + scaled[:, lanes]
        for index, row in enumerate(rows):
            piece, at = place(index, step, part, lane_blocks)
            small_ref[piece, pl.ds(at, 1)] = row[:, lanes]
    dot_ref[...] = dots


def backward(n, inv, back_next, bspec, mspec, q_stream, keys, values, normed, tokens, prev, gain, short, gskip, tables):
    channels = tokens.shape[1]
    width = block_width(channels)
    lanes = lambda count: split_lanes(count, width)
    mats = [tables[name] for name in ("far2", "inv_near3")]
    return pl.pallas_call(
        functools.partial(backward_kernel, n, channels // LANES),
        grid=(channels // width,),
        out_shape=(jax.ShapeDtypeStruct((TOK, channels), f32), jax.ShapeDtypeStruct((8, channels), f32),
                   jax.ShapeDtypeStruct((n, 2, LANES), f32), jax.ShapeDtypeStruct((TOK, LANES), f32)),
        in_specs=[whole(3, 8, TOK), lanes(TOK), lanes(256), lanes(256), lanes(TOK), lanes(TOK), lanes(TOK), lanes(136), lanes(TOK), lanes(TOK),
                  lanes(1), lanes(9), lanes(1)] + [whole(*mat.shape) for mat in mats],
        out_specs=[lanes(TOK), lanes(8), whole(n, 2, LANES), whole(TOK, LANES)],
        scratch_shapes=[pltpu.VMEM((144, width), f32)] * 3,
        name="backward",
    )(inv, back_next, bspec, mspec, q_stream, keys, values, normed, tokens, prev, gain, short, gskip, *mats)


def final_kernel(n, n_tp, total, gn_ref, tail_ref, dot_ref, small_ref, tile_ref, fsum_ref, rows_ref, tok_ref, gain_ref, inv_ref,
                 tok_out, medium_out, small_out, skip_out, res_out, decay_out,
                 medium_in, fin, fin_in, tail_in, small_in, small_sum, small_all, dots, dots_in,
                 msend, mrecv, ssend, srecv, asend, arecv, dsend, drecv, fsend, frecv, tsend, trecv):
    me = lax.axis_index("ctx")
    tp = lax.axis_index("tp")
    channels = gn_ref.shape[1]
    lane_blocks = channels // LANES
    barrier = pltpu.get_barrier_semaphore()
    greet(barrier, n, "ctx")
    greet(barrier, n_tp, "tp")
    mine = rows_ref[me]
    res, rate = mine[0:2], mine[2:4]
    first, second = fsum_ref[0:2], fsum_ref[2:4]
    root = jnp.sqrt(rate)
    fin[0:2] = root * first
    fin[2:4] = res / (n * TOK) * (first / (2.0 * root) - root * second)
    pl.semaphore_wait(barrier, n - 1 + n_tp - 1)

    tail_copy = send(tail_ref, tail_in, tsend, trecv, ctx=lax.rem(me + n - 1, n))
    tail_copy.start()

    def small_copy(d):
        peer = lax.rem(me + d, n)
        return send(small_ref.at[peer], small_in.at[d], ssend.at[d], srecv.at[d], ctx=peer)

    def medium_copy(d):
        return send(tile_ref, medium_in.at[me], msend.at[d], mrecv.at[d], ctx=lax.rem(me + d, n))

    def fin_copy(d):
        return send(fin, fin_in.at[me], fsend.at[d], frecv.at[d], ctx=lax.rem(me + d, n))

    def all_copy(d):
        return send(small_sum, small_all.at[me], asend.at[d], arecv.at[d], ctx=lax.rem(me + d, n))

    def dot_copy(d):
        return send(dots, dots_in.at[d], dsend.at[d], drecv.at[d], tp=lax.rem(tp + d, n_tp))

    each(1, n, lambda d: small_copy(d).start())

    def start(d):
        medium_copy(d).start()
        fin_copy(d).start()

    each(1, n, start)
    medium_in[me] = tile_ref[...]
    fin_in[me] = fin[...]

    tail_copy.wait()
    extra = jnp.where(me < n - 1, tail_in[...], 0.0)
    gn_last = gn_ref[TOK - 8:TOK] + extra
    tail_dot = jnp.sum(extra * gain_ref[...] * tok_ref[TOK - 16:TOK].astype(f32)[8:16], axis=1, keepdims=True)
    column = jnp.sum(dot_ref[...], axis=1, keepdims=True)
    column = jnp.concatenate([column[:TOK - 8], column[TOK - 8:] + tail_dot], 0)
    dots[...] = jnp.broadcast_to(to_row(column), dots.shape)
    for d in range(1, n_tp):
        dot_copy(d).start()

    def add(d, sums):
        small_copy(d).wait()
        return sums + small_in[d]

    small_sum[...] = lax.fori_loop(1, n, add, small_ref[me])
    each(1, n, lambda d: all_copy(d).start())
    small_all[me] = small_sum[...]

    dot_row = dots[...]
    for d in range(1, n_tp):
        dot_copy(d).wait()
        dot_row = dot_row + dots_in[d]
    inv_row = inv_ref[0]
    factor = to_column((inv_row * inv_row * inv_row * dot_row / total)[0:1])
    inv = to_column(inv_row[0:1])
    for block in range(lane_blocks):
        lanes = slice(block * LANES, (block + 1) * LANES)
        gn = jnp.concatenate([gn_ref[0:TOK - 8, lanes], gn_last[:, lanes]], 0)
        tok_out[:, lanes] = (inv * (gn * gain_ref[:, lanes]) - tok_ref[:, lanes].astype(f32) * factor).astype(bf16)

    def finish(d):
        medium_copy(d).wait()
        fin_copy(d).wait()

    each(1, n, finish)

    def spread(i):
        medium_out[tile_of(i, lane_blocks)] = medium_in[i].astype(f32)

    each(0, n, spread)
    offset = 16 * lax.rem(me, 8)
    select = (lax.broadcasted_iota(jnp.int32, (16, LANES), 0) + offset == lax.broadcasted_iota(jnp.int32, (16, LANES), 1)).astype(f32)
    home = me // 8
    pick = lambda left, right: lax.dot_general(left, right, (((1,), (1,)), ((), ())), precision=HIGHEST, preferred_element_type=f32)
    res_rows, decay_rows = [], []
    for m in range(MODES):
        row = m * lane_blocks + home
        res_rows.append(fin_in[row // 2, pl.ds(row % 2, 1)])
        decay_rows.append(fin_in[row // 2, pl.ds(2 + row % 2, 1)])
    res_out[...] = pick(select, jnp.concatenate(res_rows, 0))
    decay_out[...] = pick(select, jnp.concatenate(decay_rows, 0))
    each(1, n, lambda d: all_copy(d).wait())
    for row in range(10):
        for block in range(lane_blocks):
            index = row * lane_blocks + block
            small_out[row:row + 1, block * LANES:(block + 1) * LANES] = small_all[index // 2, pl.ds(index % 2, 1)]
    row = 10 * lane_blocks + home
    skip_row = small_all[row // 2, pl.ds(row % 2, 1)]
    skip_out[...] = pick(jnp.broadcast_to(skip_row, (8, LANES)), select)
    for d in range(1, n_tp):
        pass


def final(n, n_tp, total, gn, tail, dots, small, tile, fsum, rows, tokens, gain, inv):
    channels = tokens.shape[1]
    dma = pltpu.SemaphoreType.DMA
    return pl.pallas_call(
        functools.partial(final_kernel, n, n_tp, total),
        out_shape=(jax.ShapeDtypeStruct((TOK, channels), bf16), jax.ShapeDtypeStruct((TOK, channels), f32), jax.ShapeDtypeStruct((10, channels), f32),
                   jax.ShapeDtypeStruct((8, 16), f32), jax.ShapeDtypeStruct((16, MODES), f32), jax.ShapeDtypeStruct((16, MODES), f32)),
        in_specs=[VMEM_SPEC] * 10,
        out_specs=[VMEM_SPEC] * 6,
        scratch_shapes=[
            pltpu.VMEM((n, 16, LANES), bf16), pltpu.VMEM((4, LANES), f32), pltpu.VMEM((n, 4, LANES), f32), pltpu.VMEM((8, channels), f32),
            pltpu.VMEM((n, 2, LANES), f32), pltpu.VMEM((2, LANES), f32), pltpu.VMEM((n, 2, LANES), f32),
            pltpu.VMEM((8, TOK), f32), pltpu.VMEM((n_tp, 8, TOK), f32),
        ] + [dma((n,))] * 6 + [dma((n_tp,))] * 2 + [dma((n,))] * 2 + [dma, dma],
        compiler_params=pltpu.CompilerParams(collective_id=4, has_side_effects=True),
        name="final",
    )(gn, tail, dots, small, tile, fsum, rows, tokens, gain, inv)


def per_device(tokens, norm_gain, short_filter, medium_filter, residues, decay_rate, skip_gain, grad_out):
    channels = tokens.shape[1]
    n, n_tp = lax.axis_size("ctx"), lax.axis_size("tp")
    total = channels * n_tp
    tables = {name: jnp.asarray(table) for name, table in transform_tables().items()}
    order = jnp.asarray(lane_orders())
    gain = norm_gain.reshape(1, channels)
    short = short_filter.reshape(9, channels)
    inv, prev, prev2, par = entry(tokens, residues, decay_rate, skip_gain, total)
    query, keys, values, normed, gspec, mspec, conv, backl, gskip, sr, aux, rows = forward(
        inv, tokens, prev, prev2, gain, short, medium_filter, par, grad_out, tables, order)
    hq = states(sr, rows)
    block_out, back, q_stream, medium_part, bspec, fs = middle(hq, sr, aux, rows, conv, backl, query, grad_out, gspec, tables)
    back_next, tile, fsum = reduce_medium(back, medium_part, fs)
    gn, tail, small, dots = backward(n, inv, back_next, bspec, mspec, q_stream, keys, values, normed, tokens, prev, gain, short, gskip, tables)
    grad_tokens, grad_medium, small_out, skip_out, grad_residues, grad_decay = final(
        n, n_tp, total, gn, tail, dots, small, tile, fsum, rows, tokens, gain, inv)
    return (block_out, grad_tokens, small_out[9], small_out[:9].reshape(3, 3, channels), grad_medium, skip_out[0], grad_residues, grad_decay)


def solution(mesh):
    cols = P(("tp", "ctx"), None)
    specs = (P("ctx", "tp"), P("tp"), P(None, None, "tp"), P(None, "tp"), cols, cols, P(("tp", "ctx")), P("ctx", "tp"))
    outs = (P("ctx", "tp"), P("ctx", "tp"), P("tp"), P(None, None, "tp"), P(None, "tp"), P(("tp", "ctx")), cols, cols)
    return jax.shard_map(per_device, mesh=mesh, in_specs=specs, out_specs=outs, check_vma=False)
```

time: 494 us -> 137 us (0.28)
  the two profiles are of different devices: /device:TPU:8 before, /device:TPU:1 now
where the time goes in v1:
time: 137 us; the launch traced here: 136 us
  Pallas kernels  126 us (92%)
  local copies, waits for them, and re-layouts  9.29 us (7%)
    pallas_call x1, Pallas kernels, final(): pl.pallas_call(functools.partial(final_kernel, n, n_tp, total), out_shape...  28.5 us
    pallas_call x1, Pallas kernels, entry(): pl.pallas_call(functools.partial(entry_kernel, n, n_tp, total), out_shape...  25.6 us
    pallas_call x1, Pallas kernels, states(): pl.pallas_call(functools.partial(states_kernel, n), out_shape=jax.ShapeDt...  25.3 us
    pallas_call x1, Pallas kernels, reduce_medium(): pl.pallas_call(functools.partial(reduce_kernel, n), out_shape=(jax.ShapeD...  21.9 us
    pallas_call x1, Pallas kernels, forward(): pl.pallas_call(functools.partial(forward_kernel, n, lane_blocks), grid=(c...  12.1 us
    pallas_call x1, Pallas kernels, middle(): pl.pallas_call(functools.partial(middle_kernel, channels // LANES), grid=...  6.74 us
    pallas_call x1, Pallas kernels, backward(): pl.pallas_call(functools.partial(backward_kernel, n, channels // LANES),...  6.04 us
    unnamed x10, local copies, waits for them, and re-layouts  3.77 us

profile of v1, /device:TPU:1, one launch (start us, length us, event | category | flops | bytes accessed | tf_op | source)
XLA Modules:
  0.0 136.1 jit_solution(14538756367107218429)
XLA Ops:
  0.6 1.5 %reshape.30.sf_ref = f32[9,1024]{1,0:T(8,128)} reshape(f32[3,3,1024]{2,1,0:T(4,128)} %param.17) | data formatting | bytes 73728 | tf_op jit(solution)/shard_map/reshape | solution.py:721
  2.1 25.6 %entry.1 = (f32[3,8,128]{2,1,0:T(8,128)}, bf16[128,1024]{1,0:T(8,128)(2,1)}, bf16[16,1024]{1,0:T(8,128)(2,1)}, f32[64,8,128]{2,1,0:T(8,128)}) custom-call(bf16[128,1024]{1,0:T(8,128)(2,1)} %tok_ref.7, f32[16,16]{1,0:T(8,128)} %res_ref.1, f32[16,16]{1,0:T(8,128)} %rate_ref.1, f32[1,16]{1,0:T(1,128)} %bitcast.11), custom_call_target="tpu_custom_call" | custom-call | tf_op jit(solution)/shard_map/entry/pallas_call | solution.py:180
  27.7 12.1 %forward.1 = (f32[128,1024]{1,0:T(8,128)}, f32[128,1024]{1,0:T(8,128)}, f32[128,1024]{1,0:T(8,128)}, f32[136,1024]{1,0:T(8,128)}, f32[256,1024]{1,0:T(8,128)}, /...) custom-call(f32[3,8,128]{2,1,0:T(8,128)} %get-tuple-element.43.inv_r, ...), custom_call_target="tpu_custom_call" | custom-call | tf_op jit(solution)/shard_map/forward/pallas_call | solution.py:338
  39.8 25.3 %states.1.hq_ref = f32[64,4,128]{2,1,0:T(4,128)} custom-call(f32[64,4,128]{2,1,0:T(4,128)} %get-tuple-element.47.sr_ref, f32[64,8,128]{2,1,0:T(8,128)} %get-tuple-element.48.rows_ref), custom_call_target="tpu_custom_call" | custom-call | tf_op jit(solution)/shard_map/states/pallas_call | solution.py:389
  65.1 6.7 %middle.1 = (bf16[128,1024]{1,0:T(8,128)(2,1)}, bf16[128,1024]{1,0:T(8,128)(2,1)}, bf16[128,1024]{1,0:T(8,128)(2,1)}, bf16[128,1024]{1,0:T(8,128)(2,1)}, f32[256,1024]{1,0:T(8,128)}, /*index=5*/f32[64,4,128]{2,1,0:T(4,128)}) custom-call(f32[64,4,128]{2,1,0:T(4,128)} %states.1.hq_ref, f32[64,4,128]{2,1,0:T(4,128)} %get-tuple-element.47.sr_ref, ...), custom_call_target="tpu_custom_call" | custom-call | tf_op jit(solution)/shard_map/middle/pallas_call | solution.py:452
  71.8 21.9 %reduce_medium.1 = (bf16[128,1024]{1,0:T(8,128)(2,1)}, bf16[16,128]{1,0:T(8,128)(2,1)}, f32[4,128]{1,0:T(4,128)}) custom-call(bf16[128,1024]{1,0:T(8,128)(2,1)} %get-tuple-element.55.back_ref, bf16[128,1024]{1,0:T(8,128)(2,1)} %get-tuple-element.56.medium_ref, f32[64,4,128]{2,1,0:T(4,128)} %get-tuple-element.57.fs_ref), custom_call_target="tpu_custom_call" | custom-call | tf_op jit(solution)/shard_map/reduce_medium/pallas_call | solution.py:507
  93.7 6.0 %backward.1 = (f32[128,1024]{1,0:T(8,128)}, f32[8,1024]{1,0:T(8,128)}, f32[64,2,128]{2,1,0:T(2,128)}, f32[128,128]{1,0:T(8,128)}) custom-call(f32[3,8,128]{2,1,0:T(8,128)} %get-tuple-element.43.inv_ref, bf16[128,1024]{1,0:T(8,128)(2,1)} %get-tuple-element.58.next_ref, f32[256,1024]{1,0:T(8,128)} %get-tuple-element.59.bspec_ref, ...), custom_call_target="tpu_custom_call" | custom-call | tf_op jit(solution)/shard_map/backward/pallas_call | solution.py:571
  99.7 28.5 %final.1 = (bf16[128,1024]{1,0:T(8,128)(2,1)}, f32[128,1024]{1,0:T(8,128)}, f32[10,1024]{1,0:T(8,128)}, f32[8,16]{1,0:T(8,128)}, f32[16,16]{1,0:T(8,128)}, /*index=5*/f32[16,16]{1,0:T(8,128)}) custom-call(f32[128,1024]{1,0:T(8,128)} %get-tuple-element.66.gn_ref, f32[8,1024]{1,0:T(8,128)} %get-tuple-element.67.tail_ref, ...), custom_call_target="tpu_custom_call" | custom-call | tf_op jit(solution)/shard_map/final/pallas_call | solution.py:698
  128.3 0.0 copy-start
  128.3 1.2 slice_bitcast_fusion
  129.5 1.4 slice.9
  130.9 1.5 %reshape.31 = f32[3,3,1024]{2,1,0:T(4,128)} reshape(f32[9,1024]{1,0:T(8,128)} %bitcast.6) | data formatting | bytes 73728 | tf_op jit(solution)/shard_map/reshape | solution.py:731
  132.3 1.7 %copy.27 = bf16[128,1024]{1,0:T(8,128)(2,1)} copy(bf16[128,1024]{1,0:T(8,128)(2,1)} %get-tuple-element.87) | data formatting | bytes 524288
  134.0 0.0 copy-done
  134.0 0.0 copy-start.2
  134.0 0.8 copy.28
  134.8 0.0 copy-done.2
  134.8 0.0 copy-start.1
  134.8 0.6 copy.29
  135.4 0.1 copy-done.1
  135.5 0.6 copy.30
Async XLA Ops:
  128.3 5.8 %copy-start = (f32[128,1024]{1,0:T(8,128)S(1)}, f32[128,1024]{1,0:T(8,128)}, u32[]{:S(2)}) copy-start(f32[128,1024]{1,0:T(8,128)} %get-tuple-element.90) | copy-start | bytes 1572868
  134.0 0.8 copy-start.2
  134.8 0.7 copy-start.1

commit v2 on v1

v2 whole, which is shorter than its diff:
```python
import functools
import math

import jax
import jax.numpy as jnp
import ml_dtypes
import numpy as np
from jax import lax
from jax.experimental import pallas as pl
from jax.experimental.pallas import tpu as pltpu
from jax.sharding import PartitionSpec as P

EPSILON = 1e-06
HIGHEST = lax.Precision.HIGHEST
MESH = pl.DeviceIdType.MESH
TOK = 128
MODES = 16
LANES = 128
f32 = jnp.float32
bf16 = jnp.bfloat16
VMEM_SPEC = pl.BlockSpec(memory_space=pltpu.VMEM)


def transform_tables():
    freq = 2 * np.arange(TOK)[:, None] + 1
    angle = np.pi / 256.0 * ((freq * np.arange(256)[None, :]) % 512)
    table = np.concatenate([np.cos(angle), -np.sin(angle)], 0)

    def two(matrix):
        high = matrix.astype(ml_dtypes.bfloat16)
        return high, (matrix - high.astype(np.float64)).astype(ml_dtypes.bfloat16)

    high, low = two(table)
    near, far = slice(0, TOK), slice(TOK, 256)
    inv_near, inv_near_low = two(table[:, near].T / 128.0)
    inv_far, inv_far_low = two(table[:, far].T / 128.0)
    cat = lambda *parts: np.concatenate(parts, 1)
    return {
        "whole2": cat(high, low),
        "near2": cat(high[:, near], low[:, near]),
        "far2": cat(high[:, far], low[:, far]),
        "near3": cat(high[:, near], high[:, near], low[:, near]),
        "inv_near3": cat(inv_near, inv_near, inv_near_low),
        "inv_far3": cat(inv_far, inv_far, inv_far_low),
    }


def lane_orders():
    order = np.zeros((2, 64, LANES), np.float32)
    for half in range(2):
        for row in range(64):
            order[half, row, 16 * (row // 8) + 8 * half + row % 8] = 1.0
    return order


def dot2(table, data):
    return jnp.dot(table, jnp.concatenate([data, data], 0), preferred_element_type=f32)


def dot3(table, data):
    high = data.astype(bf16)
    low = (data - high.astype(f32)).astype(bf16)
    return jnp.dot(table, jnp.concatenate([high, low, high], 0), preferred_element_type=f32)


def halves(spectrum):
    return spectrum[:TOK], spectrum[TOK:]


def product(first, second):
    (a, b), (c, d) = halves(first), halves(second)
    return jnp.concatenate([a * c - b * d, a * d + b * c], 0)


def product_conj(first, second):
    (a, b), (c, d) = halves(first), halves(second)
    return jnp.concatenate([a * c + b * d, b * c - a * d], 0)


def eye(size):
    return (lax.broadcasted_iota(jnp.int32, (size, size), 0) == lax.broadcasted_iota(jnp.int32, (size, size), 1)).astype(f32)


def to_column(row):
    return jnp.sum(eye(row.shape[1]) * row, axis=1, keepdims=True)


def to_row(column):
    return jnp.sum(eye(column.shape[0]) * column, axis=0, keepdims=True)


def place(row, step, part, lane_blocks):
    if lane_blocks == 1:
        return row // 2, row % 2
    return row * (lane_blocks // 2) + step, part


def greet(barrier, count, axis):
    me = lax.axis_index(axis)

    def body(d, carry):
        pl.semaphore_signal(barrier, inc=1, device_id={axis: lax.rem(me + d, count)}, device_id_type=MESH)
        return carry

    lax.fori_loop(1, count, body, 0)


def send(src, dst, send_sem, recv_sem, **where):
    return pltpu.make_async_remote_copy(src, dst, send_sem, recv_sem, device_id=where, device_id_type=MESH)


def each(first, last, work):
    def body(d, carry):
        work(d)
        return carry

    lax.fori_loop(first, last, body, 0)


def powers(rate_row, exponents):
    return jnp.exp(-rate_row * exponents)


def sublanes():
    return lax.broadcasted_iota(jnp.int32, (8, LANES), 0).astype(f32)


def horner(blocks, eighth):
    total = blocks[-1]
    moment = jnp.zeros_like(total)
    for block in blocks[-2::-1]:
        shifted = eighth * total
        moment = eighth * moment + shifted
        total = shifted + block
    return total, moment


def down(values):
    return jnp.sum(values, axis=0, keepdims=True)


def lane_parts(width):
    return [(part, slice(part * LANES, (part + 1) * LANES)) for part in range(width // LANES)]


def eight(rate):
    return jnp.broadcast_to(jnp.exp(-8.0 * rate), (8, LANES))


def row_blocks(ref, lanes):
    return [ref[8 * b:8 * b + 8, lanes] for b in range(16)]


def signals_block(me, inv_ref, tok_ref, prev_ref, prev2_ref, gain_ref, sf_ref, mf_ref, gout_ref, whole2, near3, inv_far3,
                  q_ref, k_ref, v_ref, normed_ref, gspec_ref, mspec_ref, gskip_ref, sig, grd, ext):
    gain = gain_ref[...]

    def normed_of(values, inv_row, live):
        scale = to_column(inv_row)[TOK - values.shape[0]:]
        rounded = (values.astype(f32) * scale * gain).astype(bf16).astype(f32)
        return jnp.where(live, rounded, 0.0)

    ext[0:16] = normed_of(prev2_ref[...], inv_ref[2, 0:1], me >= 2)
    ext[16:144] = normed_of(prev_ref[...], inv_ref[1, 0:1], me >= 1)
    ext[144:272] = normed_of(tok_ref[...], inv_ref[0, 0:1], me >= 0)
    normed_ref[...] = ext[136:272]

    def stream(s, first, count):
        total = sf_ref[s, 0:1] * ext[first:first + count]
        for j in range(1, 3):
            total = total + sf_ref[s, j:j + 1] * ext[first - j:first - j + count]
        return total

    query = stream(0, 144, TOK)
    q_ref[...] = query
    keys = stream(1, 16, 256)
    values = stream(2, 16, 256)
    k_ref[...] = keys[TOK:]
    v_ref[...] = values[TOK:]
    gated = (keys * values).astype(bf16)
    gspec = dot2(whole2[...], gated)
    mspec = dot3(near3[...], mf_ref[...])
    gspec_ref[...] = gspec
    mspec_ref[...] = mspec
    sig[...] = dot3(inv_far3[...], product(gspec, mspec)).astype(bf16).astype(f32)
    grd[...] = (gout_ref[...].astype(f32) * query).astype(bf16).astype(f32)
    gskip_ref[...] = down(sig[...] * grd[...])


def sums_block(step, lane_blocks, par_ref, order_ref, sig, grd, sr_ref, aux_ref, rows_ref, skip_ref):
    r = sublanes()
    for part, lanes in lane_parts(sig.shape[1]):
        packed = par_ref[8 * part:8 * part + 8].reshape(64, LANES).T
        even = jnp.dot(packed, order_ref[0], precision=HIGHEST, preferred_element_type=f32)
        odd = jnp.dot(packed, order_ref[1], precision=HIGHEST, preferred_element_type=f32)
        res = even[0:16] + odd[16:32]
        rate = even[32:48] + odd[48:64]
        skip_ref[0:1, lanes] = even[64:65] + odd[65:66]
        chunk = jnp.exp(-float(TOK) * rate)
        for m in range(MODES):
            piece, row = place(m, step, part, lane_blocks)
            rows_ref[piece, pl.ds(row, 1)] = res[m:m + 1]
            rows_ref[piece, pl.ds(2 + row, 1)] = rate[m:m + 1]
            rows_ref[piece, pl.ds(4 + row, 1)] = chunk[m:m + 1]
            single = rate[m:m + 1]
            rising = powers(single, r)
            falling = powers(single, 7.0 - r)
            total, moment = horner(row_blocks(sig, lanes)[::-1], eight(single))
            sr_ref[piece, pl.ds(row, 1)] = down(falling * total)
            aux_ref[piece, pl.ds(row, 1)] = down(falling * (8.0 * moment + (7.0 - r) * total))
            total, moment = horner(row_blocks(grd, lanes), eight(single))
            sr_ref[piece, pl.ds(2 + row, 1)] = down(rising * total)
            aux_ref[piece, pl.ds(2 + row, 1)] = down(rising * (8.0 * moment + r * total))


def local_block(step, lane_blocks, rows_ref, skip_ref, sig, grd, near2, near3, inv_near3, conv_ref, back_ref, aux_ref, kern, kgr):
    r = sublanes()
    for part, lanes in lane_parts(sig.shape[1]):
        eighths, running = [], []
        for m in range(MODES):
            piece, row = place(m, step, part, lane_blocks)
            rate = rows_ref[piece, pl.ds(2 + row, 1)]
            eighths.append(eight(rate))
            running.append(rows_ref[piece, pl.ds(row, 1)] * jnp.sqrt(rate) * powers(rate, r))
        for block in range(16):
            total = running[0]
            for m in range(1, MODES):
                total = total + running[m]
            if block == 0:
                total = total + jnp.where(r == 0.0, skip_ref[0:1, lanes], 0.0)
            kern[8 * block:8 * block + 8, lanes] = total
            running = [value * eighth for value, eighth in zip(running, eighths)]
    kspec = dot3(near3[...], kern[...])
    uspec = dot2(near2[...], sig[...].astype(bf16))
    cspec = dot2(near2[...], grd[...].astype(bf16))
    conv_ref[...] = dot3(inv_near3[...], product(kspec, uspec))
    back_ref[...] = dot3(inv_near3[...], product_conj(cspec, kspec))
    kgr[...] = dot3(inv_near3[...], product_conj(cspec, uspec))
    for part, lanes in lane_parts(sig.shape[1]):
        for m in range(MODES):
            piece, row = place(m, step, part, lane_blocks)
            rate = rows_ref[piece, pl.ds(2 + row, 1)]
            rising = powers(rate, r)
            total, moment = horner(row_blocks(kgr, lanes), eight(rate))
            aux_ref[piece, pl.ds(4 + row, 1)] = down(rising * total)
            aux_ref[piece, pl.ds(6 + row, 1)] = down(rising * (8.0 * moment + r * total))


def back_block(step, lane_blocks, hq_ref, rows_ref, local_ref, back_ref):
    r = sublanes()
    for part, lanes in lane_parts(local_ref.shape[1]):
        eighths, behind = [], []
        for m in range(MODES):
            piece, row = place(m, step, part, lane_blocks)
            take = lambda ref, at: ref[piece, pl.ds(at + row, 1)]
            rate = take(rows_ref, 2)
            eighths.append(eight(rate))
            behind.append(take(rows_ref, 0) * jnp.sqrt(rate) * take(hq_ref, 2) * powers(rate, 8.0 - r))
        for block in range(15, -1, -1):
            total = local_ref[8 * block:8 * block + 8, lanes]
            for m in range(MODES):
                total = total + behind[m]
            local_ref[8 * block:8 * block + 8, lanes] = total
            behind = [value * eighth for value, eighth in zip(behind, eighths)]
    back_ref[...] = local_ref[...].astype(bf16)


def conv_block(step, lane_blocks, hq_ref, sr_ref, aux_ref, rows_ref, local_ref, back_ref, q_ref, gout_ref, gspec_ref,
               near2, inv_near3, out_ref, stream_ref, medium_ref, bspec_ref, fs_ref):
    r = sublanes()
    width = q_ref.shape[1]
    for part, lanes in lane_parts(width):
        eighths, ahead = [], []
        for m in range(MODES):
            piece, row = place(m, step, part, lane_blocks)
            take = lambda ref, at: ref[piece, pl.ds(at + row, 1)]
            res, rate, chunk = take(rows_ref, 0), take(rows_ref, 2), take(rows_ref, 4)
            state, future, near = take(hq_ref, 0), take(hq_ref, 2), take(sr_ref, 2)
            single = jnp.exp(-rate)
            fs_ref[piece, pl.ds(row, 1)] = take(aux_ref, 4) + single * near * state
            fs_ref[piece, pl.ds(2 + row, 1)] = take(aux_ref, 6) + single * (
                (near + take(aux_ref, 2)) * state + take(aux_ref, 0) * future + float(TOK) * chunk * state * future)
            eighths.append(eight(rate))
            ahead.append(res * jnp.sqrt(rate) * state * powers(rate, r + 1.0))
        for block in range(16):
            total = local_ref[8 * block:8 * block + 8, lanes]
            for m in range(MODES):
                total = total + ahead[m]
            local_ref[8 * block:8 * block + 8, lanes] = total
            ahead = [value * eighth for value, eighth in zip(ahead, eighths)]
    conv = local_ref[...].astype(bf16).astype(f32)
    out_ref[...] = (q_ref[...] * conv).astype(bf16)
    stream_ref[...] = (gout_ref[...].astype(f32) * conv).astype(bf16)
    bspec = dot2(near2[...], back_ref[...])
    bspec_ref[...] = bspec
    sign = (1 - 2 * (lax.broadcasted_iota(jnp.int32, (TOK, width), 0) % 2)).astype(f32)
    real, imag = halves(bspec)
    late = jnp.concatenate([sign * imag, -sign * real], 0)
    medium_ref[...] = dot3(inv_near3[...], product_conj(late, gspec_ref[...])).astype(bf16)


def backward_block(step, me, n, lane_blocks, inv_ref, next_ref, bspec_ref, mspec_ref, q_stream, k_ref, v_ref, normed_ref, tok_ref, prev_ref,
                   gain_ref, sf_ref, gskip_ref, far2, inv_near3, gn_ref, tail_ref, small_ref, dot_ref, pads):
    width = tok_ref.shape[1]
    later = jnp.where(me < n - 1, next_ref[...].astype(f32), 0.0).astype(bf16)
    spec = bspec_ref[...] + dot2(far2[...], later)
    grad_gated = dot3(inv_near3[...], product_conj(spec, mspec_ref[...]))
    streams = [
        q_stream[...].astype(f32),
        (grad_gated * v_ref[...]).astype(bf16).astype(f32),
        (grad_gated * k_ref[...]).astype(bf16).astype(f32),
    ]
    total = jnp.zeros((136, width), f32)
    rows = []
    for s in range(3):
        pad = pads.at[s]
        pad[0:8] = jnp.zeros((8, width), f32)
        pad[8:136] = streams[s]
        pad[136:144] = jnp.zeros((8, width), f32)
        for j in range(3):
            total = total + sf_ref[s, j:j + 1] * pad[j:j + 136]
            rows.append(down(streams[s] * normed_ref[8 - j:136 - j]))
    tail = jnp.where(me >= 1, total[0:8], 0.0)
    grad_normed = total[8:136]
    gn_ref[...] = grad_normed
    tail_ref[...] = tail
    wide = tok_ref[...].astype(f32)
    inv = to_column(inv_ref[0, 0:1])
    before = to_column(inv_ref[1, 0:1])[TOK - 8:]
    rows.append(down(grad_normed * wide * inv) + down(tail * prev_ref[TOK - 16:TOK].astype(f32)[8:16] * before))
    rows.append(gskip_ref[...])
    scaled = grad_normed * gain_ref[...] * wide
    dots = dot_ref[...]
    for part, lanes in lane_parts(width):
        dots = dots + scaled[:, lanes]
        for index, row in enumerate(rows):
            piece, at = place(index, step, part, lane_blocks)
            small_ref[piece, pl.ds(at, 1)] = row[:, lanes]
    dot_ref[...] = dots


def tile_of(index, lane_blocks):
    rows = pl.multiple_of((index // lane_blocks) * 16, 16)
    lanes = pl.multiple_of((index % lane_blocks) * LANES, LANES)
    return (pl.ds(rows, 16), pl.ds(lanes, LANES))


TABLES = ("whole2", "near2", "far2", "near3", "inv_near3", "inv_far3")
INPUTS = ("tok", "gout", "res", "rate", "skipg", "gain", "sf", "mf", "order") + TABLES
OUTPUTS = ("out", "gtok", "medium_all", "small_all", "fin_all")


def scratch_list(n, n_tp, channels, width):
    wide = lambda rows, kind=f32: pltpu.VMEM((rows, channels), kind)
    piece = lambda rows, kind=f32: pltpu.VMEM((n, rows, LANES), kind)
    row_tile = pltpu.VMEM((8, TOK), f32)
    dma = lambda *shape: pltpu.SemaphoreType.DMA(shape)
    entries = dict(
        inv=pltpu.VMEM((3, 8, TOK), f32), prev=wide(TOK, bf16), prev2=wide(16, bf16), par=piece(8),
        msg=pltpu.VMEM((8, LANES), f32), sums=row_tile, sums_in=pltpu.VMEM((n_tp, 8, TOK), f32), inv_own=row_tile,
        q=wide(TOK), k=wide(TOK), v=wide(TOK), normed=wide(136), gspec=wide(256), mspec=wide(256), bspec=wide(256),
        sig=wide(TOK), grd=wide(TOK), conv=wide(TOK), backl=wide(TOK), gskip=wide(1), skip=wide(1),
        sr=piece(4), aux=piece(8), rows=piece(8), inbox=piece(4), outbox=piece(4), hq=piece(4),
        back=wide(TOK, bf16), next=wide(TOK, bf16), qs=wide(TOK, bf16), medium=wide(TOK, bf16),
        fs=piece(4), tiles_in=piece(16, bf16), fs_in=piece(4), tile_red=pltpu.VMEM((16, LANES), bf16), fin=pltpu.VMEM((4, LANES), f32),
        gn=wide(TOK), tail=wide(8), tail_in=wide(8), small=piece(2), small_in=piece(2), small_sum=pltpu.VMEM((2, LANES), f32),
        dotacc=pltpu.VMEM((TOK, LANES), f32), dots=row_tile, dots_in=pltpu.VMEM((n_tp, 8, TOK), f32),
        ext=pltpu.VMEM((272, width), f32), kern=pltpu.VMEM((TOK, width), f32), kgr=pltpu.VMEM((TOK, width), f32), pads=pltpu.VMEM((3, 144, width), f32),
        par_s=dma(n), par_r=dma(n), sr_s=dma(n), sr_r=dma(n), hq_s=dma(n), hq_r=dma(n), tile_s=dma(n), tile_r=dma(n), fs_s=dma(n), fs_r=dma(n),
        small_s=dma(n), small_r=dma(n), med_s=dma(n), med_r=dma(n), all_s=dma(n), all_r=dma(n), fin_s=dma(n), fin_r=dma(n),
        sum_s=dma(n_tp), sum_r=dma(n_tp), dot_s=dma(n_tp), dot_r=dma(n_tp), near_s=dma(6), near_r=dma(6),
    )
    return entries


def main_kernel(n, n_tp, total, names, *refs):
    g = dict(zip(names, refs))
    me = lax.axis_index("ctx")
    tp = lax.axis_index("tp")
    channels = g["tok"].shape[1]
    width = block_width(channels)
    lane_blocks = channels // LANES
    steps = channels // width

    def blocks(work):
        def body(step, carry):
            start = pl.multiple_of(step * width, width)
            work(step, lambda name: g[name].at[:, pl.ds(start, width)])
            return carry

        lax.fori_loop(0, steps, body, 0)

    def peer(d):
        return lax.rem(me + d, n)

    def tp_peer(d):
        return lax.rem(tp + d, n_tp)

    def copies(source, target, name):
        return lambda d: send(source(d), target(d), g[name + "_s"].at[d], g[name + "_r"].at[d], ctx=peer(d))

    def near(index, source, target, where):
        return send(source, target, g["near_s"].at[index], g["near_r"].at[index], ctx=where)

    barrier = pltpu.get_barrier_semaphore()
    greet(barrier, n, "ctx")
    greet(barrier, n_tp, "tp")
    length = n * TOK
    msg = g["msg"]
    msg[...] = jnp.zeros(msg.shape, f32)
    msg[:, 0:16] = g["res"][0:8, :]
    msg[:, 16:32] = g["res"][8:16, :]
    msg[:, 32:48] = g["rate"][0:8, :] / length
    msg[:, 48:64] = g["rate"][8:16, :] / length
    skip_col = to_column(g["skipg"][...])
    msg[:, 64:65] = skip_col[0:8]
    msg[:, 65:66] = skip_col[8:16]
    wide = g["tok"][...].astype(f32)
    sums = g["sums"]
    sums[...] = jnp.broadcast_to(to_row(jnp.sum(wide * wide, axis=1, keepdims=True)), sums.shape)
    g["small"][...] = jnp.zeros(g["small"].shape, f32)
    g["dotacc"][...] = jnp.zeros(g["dotacc"].shape, f32)
    pl.semaphore_wait(barrier, n - 1 + n_tp - 1)

    sum_copy = lambda d: send(sums, g["sums_in"].at[d], g["sum_s"].at[d], g["sum_r"].at[d], tp=tp_peer(d))
    par_copy = copies(lambda d: msg, lambda d: g["par"].at[me], "par")
    tok_copy = near(0, g["tok"], g["prev"], peer(1))
    tok2_copy = near(1, g["tok"].at[pl.ds(TOK - 16, 16)], g["prev2"], peer(2))
    for d in range(1, n_tp):
        sum_copy(d).start()
    tok2_copy.start()
    tok_copy.start()
    each(1, n, lambda d: par_copy(d).start())
    g["par"][me] = msg[...]
    squares = sums[...]
    for d in range(1, n_tp):
        sum_copy(d).wait_recv()
        squares = squares + g["sums_in"][d]
    inv_own = g["inv_own"]
    inv_own[...] = lax.rsqrt(squares / total + EPSILON)
    inv_copies = [near(2, inv_own, g["inv"].at[1], peer(1)), near(3, inv_own, g["inv"].at[2], peer(2))]
    for copy in inv_copies:
        copy.start()
    g["inv"][0] = inv_own[...]
    for copy in inv_copies + [tok_copy, tok2_copy]:
        copy.wait()

    blocks(lambda step, at: signals_block(
        me, g["inv"], at("tok"), at("prev"), at("prev2"), at("gain"), g["sf"].at[:, :, pl.ds(pl.multiple_of(step * width, width), width)], at("mf"), at("gout"),
        g["whole2"], g["near3"], g["inv_far3"], at("q"), at("k"), at("v"), at("normed"), at("gspec"), at("mspec"), at("gskip"), at("sig"), at("grd"), g["ext"]))

    each(1, n, lambda d: par_copy(d).wait_recv())
    blocks(lambda step, at: sums_block(
        step, lane_blocks, g["par"].at[pl.ds(step * (8 * width // LANES), 8 * width // LANES)], g["order"], at("sig"), at("grd"), g["sr"], g["aux"], g["rows"], at("skip")))
    inbox, outbox, hq = g["inbox"], g["outbox"], g["hq"]
    sr_copy = copies(lambda d: g["sr"].at[peer(d)], lambda d: inbox.at[me], "sr")
    hq_copy = copies(lambda d: outbox.at[peer(d)], lambda d: hq.at[me], "hq")
    each(1, n, lambda d: sr_copy(d).start())
    inbox[me] = g["sr"][me]
    decay = g["rows"][me][4:6]
    each(1, n, lambda d: sr_copy(d).wait_recv())

    def scan(i, carry):
        ahead, behind = carry
        j = n - 1 - i
        outbox[i, 0:2] = ahead
        outbox[j, 2:4] = behind
        return decay * ahead + inbox[i][0:2], decay * behind + inbox[j][2:4]

    zero = jnp.zeros((2, LANES), f32)
    lax.fori_loop(0, n, scan, (zero, zero))
    each(1, n, lambda d: hq_copy(d).start())
    hq[me] = outbox[me]
    blocks(lambda step, at: local_block(
        step, lane_blocks, g["rows"], at("skip"), at("sig"), at("grd"), g["near2"], g["near3"], g["inv_near3"], at("conv"), at("backl"), g["aux"], g["kern"], g["kgr"]))
    each(1, n, lambda d: hq_copy(d).wait_recv())

    blocks(lambda step, at: back_block(step, lane_blocks, hq, g["rows"], at("backl"), at("back")))
    halo = near(4, g["back"], g["next"], peer(n - 1))
    halo.start()
    blocks(lambda step, at: conv_block(
        step, lane_blocks, hq, g["sr"], g["aux"], g["rows"], at("conv"), at("back"), at("q"), at("gout"), at("gspec"),
        g["near2"], g["inv_near3"], at("out"), at("qs"), at("medium"), at("bspec"), g["fs"]))
    tile_copy = copies(lambda d: g["medium"].at[tile_of(peer(d), lane_blocks)], lambda d: g["tiles_in"].at[d], "tile")
    fs_copy = copies(lambda d: g["fs"].at[peer(d)], lambda d: g["fs_in"].at[d], "fs")

    def start_sums(d):
        tile_copy(d).start()
        fs_copy(d).start()

    each(1, n, start_sums)
    halo.wait()
    blocks(lambda step, at: backward_block(
        step, me, n, lane_blocks, g["inv"], at("next"), at("bspec"), at("mspec"), at("qs"), at("k"), at("v"), at("normed"), at("tok"), at("prev"),
        at("gain"), g["sf"].at[:, :, pl.ds(pl.multiple_of(step * width, width), width)], at("gskip"), g["far2"], g["inv_near3"],
        at("gn"), at("tail"), g["small"], g["dotacc"], g["pads"]))

    tail_copy = near(5, g["tail"], g["tail_in"], peer(n - 1))
    tail_copy.start()
    small_copy = copies(lambda d: g["small"].at[peer(d)], lambda d: g["small_in"].at[d], "small")
    each(1, n, lambda d: small_copy(d).start())

    def add_tile(d, sums_now):
        tile_copy(d).wait()
        fs_copy(d).wait()
        return sums_now[0] + g["tiles_in"][d].astype(f32), sums_now[1] + g["fs_in"][d]

    tile, both = lax.fori_loop(1, n, add_tile, (g["medium"][tile_of(me, lane_blocks)].astype(f32), g["fs"][me]))
    g["tile_red"][...] = tile.astype(bf16)
    mine = g["rows"][me]
    res, rate = mine[0:2], mine[2:4]
    first, second = both[0:2], both[2:4]
    root = jnp.sqrt(rate)
    fin = g["fin"]
    fin[0:2] = root * first
    fin[2:4] = res / length * (first / (2.0 * root) - root * second)
    medium_copy = copies(lambda d: g["tile_red"], lambda d: g["medium_all"].at[me], "med")
    each(1, n, lambda d: medium_copy(d).start())
    g["medium_all"][me] = tile.astype(bf16)
    groups = max(lane_blocks // 2, 1)
    members = n // groups

    def fin_to(t):
        where = lax.rem(me, groups) * members + t
        return where, send(fin, g["fin_all"].at[me], g["fin_s"].at[t], g["fin_r"].at[me], ctx=where)

    def fin_from(t):
        owner = me // members + groups * t
        return owner, send(fin, g["fin_all"].at[owner], g["fin_s"].at[t], g["fin_r"].at[owner], ctx=owner)

    def start_fin(t):
        where, copy = fin_to(t)

        @pl.when(where != me)
        def _():
            copy.start()

    each(0, members, start_fin)
    g["fin_all"][me] = fin[...]

    tail_copy.wait()
    extra = jnp.where(me < n - 1, g["tail_in"][...], 0.0)
    gn_last = g["gn"][TOK - 8:TOK] + extra
    tail_dot = jnp.sum(extra * g["gain"][...] * g["tok"][TOK - 16:TOK].astype(f32)[8:16], axis=1, keepdims=True)
    column = jnp.sum(g["dotacc"][...], axis=1, keepdims=True)
    column = jnp.concatenate([column[:TOK - 8], column[TOK - 8:] + tail_dot], 0)
    dots = g["dots"]
    dots[...] = jnp.broadcast_to(to_row(column), dots.shape)
    dot_copy = lambda d: send(dots, g["dots_in"].at[d], g["dot_s"].at[d], g["dot_r"].at[d], tp=tp_peer(d))
    for d in range(1, n_tp):
        dot_copy(d).start()

    def add_small(d, sums_now):
        small_copy(d).wait()
        return sums_now + g["small_in"][d]

    small_sum = lax.fori_loop(1, n, add_small, g["small"][me])
    g["small_sum"][...] = small_sum
    all_copy = copies(lambda d: g["small_sum"], lambda d: g["small_all"].at[me], "all")
    each(1, n, lambda d: all_copy(d).start())
    g["small_all"][me] = small_sum

    dot_row = dots[...]
    for d in range(1, n_tp):
        dot_copy(d).wait()
        dot_row = dot_row + g["dots_in"][d]
    inv_row = g["inv"][0]
    factor = to_column((inv_row * inv_row * inv_row * dot_row / total)[0:1])
    inv = to_column(inv_row[0:1])
    for block in range(lane_blocks):
        lanes = slice(block * LANES, (block + 1) * LANES)
        gn = jnp.concatenate([g["gn"][0:TOK - 8, lanes], gn_last[:, lanes]], 0)
        g["gtok"][:, lanes] = (inv * (gn * g["gain"][:, lanes]) - g["tok"][:, lanes].astype(f32) * factor).astype(bf16)

    def finish_fin(t):
        where, out_copy = fin_to(t)
        owner, in_copy = fin_from(t)

        @pl.when(where != me)
        def _():
            out_copy.wait_send()

        @pl.when(owner != me)
        def _():
            in_copy.wait_recv()

    def finish(d):
        par_copy(d).wait_send()
        sr_copy(d).wait_send()
        hq_copy(d).wait_send()
        medium_copy(d).wait()
        all_copy(d).wait()

    for d in range(1, n_tp):
        sum_copy(d).wait_send()
    each(0, members, finish_fin)
    each(1, n, finish)


def finish_kernel(out_in, gtok_in, medium_in, small_in, fin_in, out_ref, gtok_ref, gain_ref, short_ref, medium_ref, skip_ref, res_ref, decay_ref):
    me = lax.axis_index("ctx")
    n = medium_in.shape[0]
    lane_blocks = out_in.shape[1] // LANES
    out_ref[...] = out_in[...]
    gtok_ref[...] = gtok_in[...]
    for i in range(n):
        row, lane = (i // lane_blocks) * 16, (i % lane_blocks) * LANES
        medium_ref[row:row + 16, lane:lane + LANES] = medium_in[i].astype(f32)
    offset = 16 * lax.rem(me, 8)
    select = (lax.broadcasted_iota(jnp.int32, (16, LANES), 0) + offset == lax.broadcasted_iota(jnp.int32, (16, LANES), 1)).astype(f32)
    home = me // 8
    pick = lambda left, right: lax.dot_general(left, right, (((1,), (1,)), ((), ())), precision=HIGHEST, preferred_element_type=f32)
    res_rows, decay_rows = [], []
    for m in range(MODES):
        row = m * lane_blocks + home
        res_rows.append(fin_in[row // 2, pl.ds(row % 2, 1)])
        decay_rows.append(fin_in[row // 2, pl.ds(2 + row % 2, 1)])
    res_ref[...] = pick(select, jnp.concatenate(res_rows, 0))
    decay_ref[...] = pick(select, jnp.concatenate(decay_rows, 0))
    for row in range(10):
        for block in range(lane_blocks):
            index = row * lane_blocks + block
            value = small_in[index // 2, index % 2:index % 2 + 1]
            if row == 9:
                gain_ref[0:1, block * LANES:(block + 1) * LANES] = value
            else:
                short_ref[row // 3, row % 3:row % 3 + 1, block * LANES:(block + 1) * LANES] = value
    row = 10 * lane_blocks + home
    skip_row = small_in[row // 2, pl.ds(row % 2, 1)]
    skip_ref[...] = pick(jnp.broadcast_to(skip_row, (8, LANES)), select)[0:1]


def block_width(channels):
    return min(256, channels)


def per_device(tokens, norm_gain, short_filter, medium_filter, residues, decay_rate, skip_gain, grad_out):
    channels = tokens.shape[1]
    n, n_tp = lax.axis_size("ctx"), lax.axis_size("tp")
    width = block_width(channels)
    made = transform_tables()
    tables = [jnp.asarray(made[name]) for name in TABLES]
    scratch = scratch_list(n, n_tp, channels, width)
    names = INPUTS + OUTPUTS + tuple(scratch)
    shape = jax.ShapeDtypeStruct
    results = pl.pallas_call(
        functools.partial(main_kernel, n, n_tp, channels * n_tp, names),
        out_shape=(shape((TOK, channels), bf16), shape((TOK, channels), bf16), shape((n, 16, LANES), bf16), shape((n, 2, LANES), f32), shape((n, 4, LANES), f32)),
        in_specs=[VMEM_SPEC] * len(INPUTS),
        out_specs=[VMEM_SPEC] * len(OUTPUTS),
        scratch_shapes=list(scratch.values()),
        compiler_params=pltpu.CompilerParams(collective_id=1, has_side_effects=True),
        name="block",
    )(tokens, grad_out, residues, decay_rate, skip_gain.reshape(1, -1), norm_gain.reshape(1, channels), short_filter, medium_filter, jnp.asarray(lane_orders()), *tables)
    small = skip_gain.shape[0]
    outs = pl.pallas_call(
        finish_kernel,
        out_shape=(shape((TOK, channels), bf16), shape((TOK, channels), bf16), shape((1, channels), f32), shape((3, 3, channels), f32),
                   shape((TOK, channels), f32), shape((1, small), f32), shape((small, MODES), f32), shape((small, MODES), f32)),
        in_specs=[VMEM_SPEC] * 5,
        out_specs=[VMEM_SPEC] * 8,
        name="finish",
    )(*results)
    block_out, grad_tokens, grad_gain, grad_short, grad_medium, grad_skip, grad_residues, grad_decay = outs
    return (block_out, grad_tokens, grad_gain.reshape(channels), grad_short, grad_medium, grad_skip.reshape(small), grad_residues, grad_decay)


def solution(mesh):
    cols = P(("tp", "ctx"), None)
    specs = (P("ctx", "tp"), P("tp"), P(None, None, "tp"), P(None, "tp"), cols, cols, P(("tp", "ctx")), P("ctx", "tp"))
    outs = (P("ctx", "tp"), P("ctx", "tp"), P("tp"), P(None, None, "tp"), P(None, "tp"), P(("tp", "ctx")), cols, cols)
    return jax.shard_map(per_device, mesh=mesh, in_specs=specs, out_specs=outs, check_vma=False)
```

time: 137 us -> 92.9 us (0.68)
  Pallas kernels: 126 us -> 92.1 us
  local copies, waits for them, and re-layouts: 9.29 us -> 0 us
    pallas_call x7 -> x2, Pallas kernels: 126 us -> 92.1 us  [the longest x1 89.9 us: per_device(): pl.pallas_call(functools.partial(main_kernel, n, n_tp, channels * n_tp, n...]
    unnamed x10 -> x0, local copies, waits for them, and re-layouts: 3.77 us -> none
    reshape x2 -> x0, local copies, waits for them, and re-layouts: 2.93 us -> none  [the longest x1 1.48 us: per_device(): small_out[:9].reshape(3, 3, channels)]
where the time goes in v2:
time: 92.9 us; the launch traced here: 92.8 us
  Pallas kernels  92.1 us (99%)
    pallas_call x1, Pallas kernels, per_device(): pl.pallas_call(functools.partial(main_kernel, n, n_tp, channels * n_tp, n...  89.9 us
    pallas_call x1, Pallas kernels, per_device(): pl.pallas_call(finish_kernel, out_shape=(shape((TOK, channels), bf16), sh...  2.25 us

profile of v2, /device:TPU:1, one launch (start us, length us, event | category | flops | bytes accessed | tf_op | source)
XLA Modules:
  0.0 92.8 jit_solution(11473927060323531259)
XLA Ops:
  0.6 89.9 %block.1 = (bf16[128,1024]{1,0:T(8,128)(2,1)}, bf16[128,1024]{1,0:T(8,128)(2,1)}, bf16[64,16,128]{2,1,0:T(8,128)(2,1)}, f32[64,2,128]{2,1,0:T(2,128)}, f32[64,4,128]{2,1,0:T(4,128)}) custom-call(bf16[128,1024]{1,0:T(8,128)(2,1)} %refs_0_.1, bf16[128,1024]{1,0:T(8,128)(2,1)} %refs_1_.1, f32[16,16]{1,0:T(8,128)} %refs_2_.1, f32[16,16]{1,0:T(8,128)} %refs_3_.1, ...), custom_call_target="tpu_custom_call" | custom-call | tf_op jit(solution)/shard_map/block/pallas_call | solution.py:646
  90.5 2.3 %finish.1 = (bf16[128,1024]{1,0:T(8,128)(2,1)}, bf16[128,1024]{1,0:T(8,128)(2,1)}, f32[1,1024]{1,0:T(1,128)}, f32[3,3,1024]{2,1,0:T(4,128)}, f32[128,1024]{1,0:T...) custom-call(bf16[128,1024]{1,0:T(8,128)(2,1)} %get-tuple-element.21.out_in, ...), custom_call_target="tpu_custom_call" | custom-call | tf_op jit(solution)/shard_map/finish/pallas_call | solution.py:656

commit v3 on v2

v3 whole, which is shorter than its diff:
```python
import functools
import types

import jax
import jax.numpy as jnp
import ml_dtypes
import numpy as np
from jax import lax
from jax.experimental import pallas as pl
from jax.experimental.pallas import tpu as pltpu
from jax.sharding import PartitionSpec as P

EPSILON = 1e-06
HIGHEST = lax.Precision.HIGHEST
MESH = pl.DeviceIdType.MESH
TOK = 128
MODES = 16
NX = 4
LANES = 128
f32 = jnp.float32
bf16 = jnp.bfloat16
VMEM_SPEC = pl.BlockSpec(memory_space=pltpu.VMEM)


def transform_tables():
    freq = 2 * np.arange(TOK)[:, None] + 1
    angle = np.pi / 256.0 * ((freq * np.arange(256)[None, :]) % 512)
    table = np.concatenate([np.cos(angle), -np.sin(angle)], 0)

    def two(matrix):
        high = matrix.astype(ml_dtypes.bfloat16)
        return high, (matrix - high.astype(np.float64)).astype(ml_dtypes.bfloat16)

    high, low = two(table)
    near, far = slice(0, TOK), slice(TOK, 256)
    inv_near, inv_near_low = two(table[:, near].T / 128.0)
    inv_far, inv_far_low = two(table[:, far].T / 128.0)
    cat = lambda *parts: np.concatenate(parts, 1)
    return dict(
        whole2=cat(high, low),
        near2=cat(high[:, near], low[:, near]),
        far2=cat(high[:, far], low[:, far]),
        near3=cat(high[:, near], high[:, near], low[:, near]),
        inv_near3=cat(inv_near, inv_near, inv_near_low),
        inv_far3=cat(inv_far, inv_far, inv_far_low),
    )


def lane_orders():
    order = np.zeros((2, 64, LANES), np.float32)
    for half in range(2):
        for row in range(64):
            order[half, row, 16 * (row // 8) + 8 * half + row % 8] = 1.0
    return order


def dot2(table, data):
    return jnp.dot(table, jnp.concatenate([data, data], 0), preferred_element_type=f32)


def dot3(table, data):
    high = data.astype(bf16)
    low = (data - high.astype(f32)).astype(bf16)
    return jnp.dot(table, jnp.concatenate([high, low, high], 0), preferred_element_type=f32)


def halves(spectrum):
    return spectrum[:TOK], spectrum[TOK:]


def product(first, second):
    (a, b), (c, d) = halves(first), halves(second)
    return jnp.concatenate([a * c - b * d, a * d + b * c], 0)


def product_conj(first, second):
    (a, b), (c, d) = halves(first), halves(second)
    return jnp.concatenate([a * c + b * d, b * c - a * d], 0)


def eye(size):
    return (lax.broadcasted_iota(jnp.int32, (size, size), 0) == lax.broadcasted_iota(jnp.int32, (size, size), 1)).astype(f32)


def to_column(row):
    return jnp.sum(eye(row.shape[1]) * row, axis=1, keepdims=True)


def to_row(column):
    return jnp.sum(eye(column.shape[0]) * column, axis=0, keepdims=True)


def place(row, step, part, lane_blocks):
    if lane_blocks == 1:
        return row // 2, row % 2
    return row * (lane_blocks // 2) + step, part


def greet(barrier, count, axis):
    me = lax.axis_index(axis)

    def body(d, carry):
        pl.semaphore_signal(barrier, inc=1, device_id={axis: lax.rem(me + d, count)}, device_id_type=MESH)
        return carry

    lax.fori_loop(1, count, body, 0)


def send(src, dst, send_sem, recv_sem, **where):
    return pltpu.make_async_remote_copy(src, dst, send_sem, recv_sem, device_id=where, device_id_type=MESH)


def each(first, last, work):
    def body(d, carry):
        work(d)
        return carry

    lax.fori_loop(first, last, body, 0)


def powers(rate_row, exponents):
    return jnp.exp(-rate_row * exponents)


def sublanes():
    return lax.broadcasted_iota(jnp.int32, (8, LANES), 0).astype(f32)


def horner(blocks, eighth):
    total = blocks[-1]
    moment = jnp.zeros_like(total)
    for block in blocks[-2::-1]:
        shifted = eighth * total
        moment = eighth * moment + shifted
        total = shifted + block
    return total, moment


def down(values):
    return jnp.sum(values, axis=0, keepdims=True)


def lane_parts(width):
    return [(part, slice(part * LANES, (part + 1) * LANES)) for part in range(width // LANES)]


def eight(rate):
    return jnp.broadcast_to(jnp.exp(-8.0 * rate), (8, LANES))


def row_blocks(ref, lanes):
    return [ref[8 * b:8 * b + 8, lanes] for b in range(16)]


def signals_block(me, inv_ref, tok_ref, prev_ref, prev2_ref, gain_ref, sf_ref, gout_ref, whole2, inv_far3,
                  q_ref, k_ref, v_ref, normed_ref, gspec_ref, mspec_ref, gskip_ref, sig, grd, ext):
    gain = gain_ref[...]

    def normed_of(values, inv_row, live):
        scale = to_column(inv_row)[TOK - values.shape[0]:]
        rounded = (values.astype(f32) * scale * gain).astype(bf16).astype(f32)
        return jnp.where(live, rounded, 0.0)

    ext[0:16] = normed_of(prev2_ref[...], inv_ref[2, 0:1], me >= 2)
    ext[16:144] = normed_of(prev_ref[...], inv_ref[1, 0:1], me >= 1)
    ext[144:272] = normed_of(tok_ref[...], inv_ref[0, 0:1], me >= 0)
    normed_ref[...] = ext[136:272]

    def stream(s, first, count):
        total = sf_ref[s, 0:1] * ext[first:first + count]
        for j in range(1, 3):
            total = total + sf_ref[s, j:j + 1] * ext[first - j:first - j + count]
        return total

    query = stream(0, 144, TOK)
    q_ref[...] = query
    keys = stream(1, 16, 256)
    values = stream(2, 16, 256)
    k_ref[...] = keys[TOK:]
    v_ref[...] = values[TOK:]
    gated = (keys * values).astype(bf16)
    gspec = dot2(whole2[...], gated)
    gspec_ref[...] = gspec
    sig[...] = dot3(inv_far3[...], product(gspec, mspec_ref[...])).astype(bf16).astype(f32)
    grd[...] = (gout_ref[...].astype(f32) * query).astype(bf16).astype(f32)
    gskip_ref[...] = down(sig[...] * grd[...])


def sums_block(step, lane_blocks, par_ref, order_ref, sig, grd, sr_ref, aux_ref, rows_ref, skip_ref):
    r = sublanes()
    for part, lanes in lane_parts(sig.shape[1]):
        packed = par_ref[8 * part:8 * part + 8].reshape(64, LANES).T
        even = jnp.dot(packed, order_ref[0], precision=HIGHEST, preferred_element_type=f32)
        odd = jnp.dot(packed, order_ref[1], precision=HIGHEST, preferred_element_type=f32)
        res = even[0:16] + odd[16:32]
        rate = even[32:48] + odd[48:64]
        skip_ref[0:1, lanes] = even[64:65] + odd[65:66]
        chunk = jnp.exp(-float(TOK) * rate)
        for m in range(MODES):
            piece, row = place(m, step, part, lane_blocks)
            rows_ref[piece, pl.ds(row, 1)] = res[m:m + 1]
            rows_ref[piece, pl.ds(2 + row, 1)] = rate[m:m + 1]
            rows_ref[piece, pl.ds(4 + row, 1)] = chunk[m:m + 1]
            single = rate[m:m + 1]
            rising = powers(single, r)
            falling = powers(single, 7.0 - r)
            total, moment = horner(row_blocks(sig, lanes)[::-1], eight(single))
            sr_ref[piece, pl.ds(row, 1)] = down(falling * total)
            aux_ref[piece, pl.ds(row, 1)] = down(falling * (8.0 * moment + (7.0 - r) * total))
            total, moment = horner(row_blocks(grd, lanes), eight(single))
            sr_ref[piece, pl.ds(2 + row, 1)] = down(rising * total)
            aux_ref[piece, pl.ds(2 + row, 1)] = down(rising * (8.0 * moment + r * total))


def local_block(step, lane_blocks, rows_ref, skip_ref, sig, grd, near2, near3, inv_near3, conv_ref, back_ref, aux_ref, kern, kgr):
    r = sublanes()
    for part, lanes in lane_parts(sig.shape[1]):
        eighths, running = [], []
        for m in range(MODES):
            piece, row = place(m, step, part, lane_blocks)
            rate = rows_ref[piece, pl.ds(2 + row, 1)]
            eighths.append(eight(rate))
            running.append(rows_ref[piece, pl.ds(row, 1)] * jnp.sqrt(rate) * powers(rate, r))
        for block in range(16):
            total = running[0]
            for m in range(1, MODES):
                total = total + running[m]
            if block == 0:
                total = total + jnp.where(r == 0.0, skip_ref[0:1, lanes], 0.0)
            kern[8 * block:8 * block + 8, lanes] = total
            running = [value * eighth for value, eighth in zip(running, eighths)]
    kspec = dot3(near3[...], kern[...])
    uspec = dot2(near2[...], sig[...].astype(bf16))
    cspec = dot2(near2[...], grd[...].astype(bf16))
    conv_ref[...] = dot3(inv_near3[...], product(kspec, uspec))
    back_ref[...] = dot3(inv_near3[...], product_conj(cspec, kspec))
    kgr[...] = dot3(inv_near3[...], product_conj(cspec, uspec))
    for part, lanes in lane_parts(sig.shape[1]):
        for m in range(MODES):
            piece, row = place(m, step, part, lane_blocks)
            rate = rows_ref[piece, pl.ds(2 + row, 1)]
            rising = powers(rate, r)
            total, moment = horner(row_blocks(kgr, lanes), eight(rate))
            aux_ref[piece, pl.ds(4 + row, 1)] = down(rising * total)
            aux_ref[piece, pl.ds(6 + row, 1)] = down(rising * (8.0 * moment + r * total))


def back_block(step, lane_blocks, hq_ref, rows_ref, local_ref, back_ref):
    r = sublanes()
    for part, lanes in lane_parts(local_ref.shape[1]):
        eighths, behind = [], []
        for m in range(MODES):
            piece, row = place(m, step, part, lane_blocks)
            take = lambda ref, at: ref[piece, pl.ds(at + row, 1)]
            rate = take(rows_ref, 2)
            eighths.append(eight(rate))
            behind.append(take(rows_ref, 0) * jnp.sqrt(rate) * take(hq_ref, 2) * powers(rate, 8.0 - r))
        for block in range(15, -1, -1):
            total = local_ref[8 * block:8 * block + 8, lanes]
            for m in range(MODES):
                total = total + behind[m]
            local_ref[8 * block:8 * block + 8, lanes] = total
            behind = [value * eighth for value, eighth in zip(behind, eighths)]
    back_ref[...] = local_ref[...].astype(bf16)


def medium_block(back_ref, gspec_ref, near2, inv_near3, medium_ref, bspec_ref):
    bspec = dot2(near2[...], back_ref[...])
    bspec_ref[...] = bspec
    sign = (1 - 2 * (lax.broadcasted_iota(jnp.int32, (TOK, back_ref.shape[1]), 0) % 2)).astype(f32)
    real, imag = halves(bspec)
    late = jnp.concatenate([sign * imag, -sign * real], 0)
    medium_ref[...] = dot3(inv_near3[...], product_conj(late, gspec_ref[...])).astype(bf16)


def conv_block(step, lane_blocks, hq_ref, sr_ref, aux_ref, rows_ref, local_ref, q_ref, gout_ref, out_ref, stream_ref, fs_ref):
    r = sublanes()
    width = q_ref.shape[1]
    for part, lanes in lane_parts(width):
        eighths, ahead = [], []
        for m in range(MODES):
            piece, row = place(m, step, part, lane_blocks)
            take = lambda ref, at: ref[piece, pl.ds(at + row, 1)]
            res, rate, chunk = take(rows_ref, 0), take(rows_ref, 2), take(rows_ref, 4)
            state, future, near = take(hq_ref, 0), take(hq_ref, 2), take(sr_ref, 2)
            single = jnp.exp(-rate)
            home = (step * (width // LANES) + part) * 8 + m // 2
            fs_ref[home, pl.ds(m % 2, 1)] = take(aux_ref, 4) + single * near * state
            fs_ref[home, pl.ds(2 + m % 2, 1)] = take(aux_ref, 6) + single * (
                (near + take(aux_ref, 2)) * state + take(aux_ref, 0) * future + float(TOK) * chunk * state * future)
            eighths.append(eight(rate))
            ahead.append(res * jnp.sqrt(rate) * state * powers(rate, r + 1.0))
        for block in range(16):
            total = local_ref[8 * block:8 * block + 8, lanes]
            for m in range(MODES):
                total = total + ahead[m]
            local_ref[8 * block:8 * block + 8, lanes] = total
            ahead = [value * eighth for value, eighth in zip(ahead, eighths)]
    conv = local_ref[...].astype(bf16).astype(f32)
    out_ref[...] = (q_ref[...] * conv).astype(bf16)
    stream_ref[...] = (gout_ref[...].astype(f32) * conv).astype(bf16)


def backward_block(me, n, inv_ref, next_ref, bspec_ref, mspec_ref, q_stream, k_ref, v_ref, normed_ref, tok_ref, prev_ref,
                   gain_ref, sf_ref, gskip_ref, far2, inv_near3, gn_ref, tail_ref, small_ref, dot_ref, pads):
    width = tok_ref.shape[1]
    later = jnp.where(me < n - 1, next_ref[...].astype(f32), 0.0).astype(bf16)
    spec = bspec_ref[...] + dot2(far2[...], later)
    grad_gated = dot3(inv_near3[...], product_conj(spec, mspec_ref[...]))
    streams = [
        q_stream[...].astype(f32),
        (grad_gated * v_ref[...]).astype(bf16).astype(f32),
        (grad_gated * k_ref[...]).astype(bf16).astype(f32),
    ]
    total = jnp.zeros((136, width), f32)
    rows = []
    for s in range(3):
        pad = pads.at[s]
        pad[0:8] = jnp.zeros((8, width), f32)
        pad[8:136] = streams[s]
        pad[136:144] = jnp.zeros((8, width), f32)
        for j in range(3):
            total = total + sf_ref[s, j:j + 1] * pad[j:j + 136]
            rows.append(down(streams[s] * normed_ref[8 - j:136 - j]))
    tail = jnp.where(me >= 1, total[0:8], 0.0)
    grad_normed = total[8:136]
    gn_ref[...] = grad_normed
    tail_ref[...] = tail
    wide = tok_ref[...].astype(f32)
    inv = to_column(inv_ref[0, 0:1])
    before = to_column(inv_ref[1, 0:1])[TOK - 8:]
    rows.append(down(grad_normed * wide * inv) + down(tail * prev_ref[TOK - 16:TOK].astype(f32)[8:16] * before))
    rows.append(gskip_ref[...])
    scaled = grad_normed * gain_ref[...] * wide
    dots = dot_ref[...]
    for part, lanes in lane_parts(width):
        dots = dots + scaled[:, lanes]
    dot_ref[...] = dots
    for index, row in enumerate(rows):
        small_ref[index // 2, index % 2:index % 2 + 1] = row


def scratch_list(n, n_tp, channels, width):
    wide = lambda rows, kind=f32: pltpu.VMEM((rows, channels), kind)
    piece = lambda rows, kind=f32: pltpu.VMEM((n, rows, LANES), kind)
    row_tile = pltpu.VMEM((8, TOK), f32)
    dma = lambda *shape: pltpu.SemaphoreType.DMA(shape)
    entries = dict(
        inv=pltpu.VMEM((3, 8, TOK), f32), prev=wide(TOK, bf16), prev2=wide(16, bf16), par=piece(8),
        msg=pltpu.VMEM((8, LANES), f32), sums=row_tile, sums_in=pltpu.VMEM((n_tp, 8, TOK), f32), inv_own=row_tile,
        q=wide(TOK), k=wide(TOK), v=wide(TOK), normed=wide(136), gspec=wide(256), mspec=wide(256), bspec=wide(256),
        sig=wide(TOK), grd=wide(TOK), conv=wide(TOK), backl=wide(TOK), gskip=wide(1), skip=wide(1),
        sr=piece(4), aux=piece(8), rows=piece(8), inbox=piece(4), outbox=piece(4), hq=piece(4),
        back=wide(TOK, bf16), next=wide(TOK, bf16), qs=wide(TOK, bf16), medium=wide(TOK, bf16),
        slabs_in=pltpu.VMEM((8, TOK, LANES), bf16), slab=pltpu.VMEM((TOK, LANES), bf16), tiles_in=pltpu.VMEM((8, 16, LANES), bf16),
        tile_red=pltpu.VMEM((16, LANES), bf16), slab_all=pltpu.VMEM((TOK, LANES), bf16),
        fs=piece(4), fs_in=pltpu.VMEM((8, 8, 4, LANES), f32), fs_slab=pltpu.VMEM((8, 4, LANES), f32), fsz_in=pltpu.VMEM((8, 4, LANES), f32), fin=pltpu.VMEM((4, LANES), f32),
        small=pltpu.VMEM((8, 2, channels), f32), small_in=pltpu.VMEM((8, 8, 2, LANES), f32), small_slab=pltpu.VMEM((8, 2, LANES), f32),
        smallz_in=pltpu.VMEM((8, 8, 2, LANES), f32), small_sum=pltpu.VMEM((8, 2, LANES), f32),
        tot=pltpu.VMEM((4, 4, LANES), f32), tots=pltpu.VMEM((NX, 4, 4, LANES), f32),
        gn=wide(TOK), tail=wide(8), tail_in=wide(8),
        dotacc=pltpu.VMEM((TOK, LANES), f32), dots=row_tile, dots_in=pltpu.VMEM((n_tp, 8, TOK), f32),
        ext=pltpu.VMEM((272, width), f32), kern=pltpu.VMEM((TOK, width), f32), kgr=pltpu.VMEM((TOK, width), f32), pads=pltpu.VMEM((3, 144, width), f32),
        par_s=dma(n), par_r=dma(n), sr_s=dma(16), sr_r=dma(16), hq_s=dma(16), hq_r=dma(16), tot_s=dma(NX), tot_r=dma(NX),
        mx_s=dma(8), mx_r=dma(8), mz_s=dma(8), mz_r=dma(8), az_s=dma(8), az_r=dma(8), ax_s=dma(8), ax_r=dma(8),
        fx_s=dma(8), fx_r=dma(8), fz_s=dma(8), fz_r=dma(8), fin_s=dma(8), fin_r=dma(8),
        sx_s=dma(8), sx_r=dma(8), sz_s=dma(8), sz_r=dma(8), bx_s=dma(8), bx_r=dma(8),
        sum_s=dma(n_tp), sum_r=dma(n_tp), dot_s=dma(n_tp), dot_r=dma(n_tp), near_s=dma(6), near_r=dma(6),
    )
    return entries


def main_kernel(n, n_tp, total, names, *refs):
    g = types.SimpleNamespace(**dict(zip(names, refs)))
    me = lax.axis_index("ctx")
    tp = lax.axis_index("tp")
    channels = g.tok.shape[1]
    width = block_width(channels)
    lane_blocks = channels // LANES
    steps = channels // width

    def blocks(work, first=0, last=steps):
        def body(step, carry):
            start = pl.multiple_of(step * width, width)
            work(step, lambda ref: ref.at[:, pl.ds(start, width)])
            return carry

        lax.fori_loop(first, last, body, 0)

    def peer(d):
        return lax.rem(me + d, n)

    def tp_peer(d):
        return lax.rem(tp + d, n_tp)

    row = n // NX
    me_x, spot = me // row, lax.rem(me, row)
    me_z, core = spot // 2, lax.rem(spot, 2)
    own_slab = 2 * me_x + core

    def row_peer(d):
        return lax.rem(spot + d, row)

    def x_peer(d):
        return lax.rem(me_x + d, NX)

    def slab_peer(d):
        return lax.rem(own_slab + d, 8)

    def z_peer(d):
        return lax.rem(me_z + d, 8)

    def in_row(d):
        return me_x * row + row_peer(d)

    def in_x(d):
        return x_peer(d) * row + spot

    def in_slab(d):
        other = slab_peer(d)
        return (other // 2) * row + me_z * 2 + lax.rem(other, 2)

    def in_z(d):
        return me_x * row + z_peer(d) * 2 + core

    def copies(source, target, sems, where=peer):
        return lambda d: send(source(d), target(d), sems[0].at[d], sems[1].at[d], ctx=where(d))

    def slab_lanes(index):
        return pl.ds(pl.multiple_of(index * LANES, LANES), LANES)

    def near(index, source, target, where):
        return send(source, target, g.near_s.at[index], g.near_r.at[index], ctx=where)

    barrier = pltpu.get_barrier_semaphore()
    greet(barrier, n, "ctx")
    greet(barrier, n_tp, "tp")
    length = n * TOK
    msg = g.msg
    msg[...] = jnp.zeros(msg.shape, f32)
    msg[:, 0:16] = g.res[0:8, :]
    msg[:, 16:32] = g.res[8:16, :]
    msg[:, 32:48] = g.rate[0:8, :] / length
    msg[:, 48:64] = g.rate[8:16, :] / length
    skip_col = to_column(g.skipg[...])
    msg[:, 64:65] = skip_col[0:8]
    msg[:, 65:66] = skip_col[8:16]
    wide = g.tok[...].astype(f32)
    sums = g.sums
    sums[...] = jnp.broadcast_to(to_row(jnp.sum(wide * wide, axis=1, keepdims=True)), sums.shape)
    g.small[...] = jnp.zeros(g.small.shape, f32)
    g.dotacc[...] = jnp.zeros(g.dotacc.shape, f32)

    def filter_spectrum(step, at):
        at(g.mspec)[...] = dot3(g.near3[...], at(g.mf)[...])

    blocks(filter_spectrum)
    pl.semaphore_wait(barrier, n - 1 + n_tp - 1)

    sum_copy = lambda d: send(sums, g.sums_in.at[d], g.sum_s.at[d], g.sum_r.at[d], tp=tp_peer(d))
    par_copy = copies(lambda d: msg, lambda d: g.par.at[me], (g.par_s, g.par_r))
    tok_copy = near(0, g.tok, g.prev, peer(1))
    tok2_copy = near(1, g.tok.at[pl.ds(TOK - 16, 16)], g.prev2, peer(2))
    for d in range(1, n_tp):
        sum_copy(d).start()
    tok2_copy.start()
    tok_copy.start()
    each(1, n, lambda d: par_copy(d).start())
    g.par[me] = msg[...]
    squares = sums[...]
    for d in range(1, n_tp):
        sum_copy(d).wait_recv()
        squares = squares + g.sums_in[d]
    inv_own = g.inv_own
    inv_own[...] = lax.rsqrt(squares / total + EPSILON)
    inv_copies = [near(2, inv_own, g.inv.at[1], peer(1)), near(3, inv_own, g.inv.at[2], peer(2))]
    for copy in inv_copies:
        copy.start()
    g.inv[0] = inv_own[...]
    for copy in inv_copies + [tok_copy, tok2_copy]:
        copy.wait()

    blocks(lambda step, at: signals_block(
        me, g.inv, at(g.tok), at(g.prev), at(g.prev2), at(g.gain), g.sf.at[:, :, pl.ds(pl.multiple_of(step * width, width), width)], at(g.gout),
        g.whole2, g.inv_far3, at(g.q), at(g.k), at(g.v), at(g.normed), at(g.gspec), at(g.mspec), at(g.gskip), at(g.sig), at(g.grd), g.ext))

    each(1, n, lambda d: par_copy(d).wait_recv())
    blocks(lambda step, at: sums_block(
        step, lane_blocks, g.par.at[pl.ds(step * (8 * width // LANES), 8 * width // LANES)], g.order, at(g.sig), at(g.grd), g.sr, g.aux, g.rows, at(g.skip)))
    inbox, outbox, hq = g.inbox, g.outbox, g.hq
    four = lambda index: pl.ds(4 * index, 4)
    sr_copy = copies(lambda d: g.sr.at[four(row_peer(d))], lambda d: inbox.at[four(spot)], (g.sr_s, g.sr_r), in_row)
    hq_copy = copies(lambda d: outbox.at[four(row_peer(d))], lambda d: hq.at[four(spot)], (g.hq_s, g.hq_r), in_row)
    tot_copy = copies(lambda d: g.tot, lambda d: g.tots.at[me_x], (g.tot_s, g.tot_r), in_x)
    each(1, row, lambda d: sr_copy(d).start())
    inbox[four(spot)] = g.sr[four(spot)]
    decay = g.rows[four(spot)][:, 4:6]
    row_decay = decay * decay
    row_decay = row_decay * row_decay
    row_decay = row_decay * row_decay
    row_decay = row_decay * row_decay
    each(1, row, lambda d: sr_copy(d).wait_recv())

    def advance(i, carry):
        ahead, behind = carry
        return decay * ahead + inbox[four(i)][:, 0:2], decay * behind + inbox[four(row - 1 - i)][:, 2:4]

    zero = jnp.zeros((4, 2, LANES), f32)
    ahead_total, behind_total = lax.fori_loop(0, row, advance, (zero, zero))
    g.tot[:, 0:2] = ahead_total
    g.tot[:, 2:4] = behind_total
    for d in range(1, NX):
        tot_copy(d).start()
    for d in range(1, NX):
        tot_copy(d).wait()
    before_row, after_row = zero, zero
    for x in range(NX):
        before_row = jnp.where(x < me_x, row_decay * before_row + g.tots[x][:, 0:2], before_row)
        y = NX - 1 - x
        after_row = jnp.where(y > me_x, row_decay * after_row + g.tots[y][:, 2:4], after_row)

    def scan(i, carry):
        j = row - 1 - i
        outbox[four(i), 0:2] = carry[0]
        outbox[four(j), 2:4] = carry[1]
        return advance(i, carry)

    lax.fori_loop(0, row, scan, (before_row, after_row))
    each(1, row, lambda d: hq_copy(d).start())
    hq[four(spot)] = outbox[four(spot)]
    blocks(lambda step, at: local_block(
        step, lane_blocks, g.rows, at(g.skip), at(g.sig), at(g.grd), g.near2, g.near3, g.inv_near3, at(g.conv), at(g.backl), g.aux, g.kern, g.kgr))
    each(1, row, lambda d: hq_copy(d).wait_recv())

    blocks(lambda step, at: back_block(step, lane_blocks, hq, g.rows, at(g.backl), at(g.back)))
    halo = near(4, g.back, g.next, peer(n - 1))
    halo.start()
    blocks(lambda step, at: medium_block(at(g.back), at(g.gspec), g.near2, g.inv_near3, at(g.medium), at(g.bspec)))
    mx_copy = copies(lambda d: g.medium.at[:, slab_lanes(slab_peer(d))], lambda d: g.slabs_in.at[d], (g.mx_s, g.mx_r), in_slab)
    each(1, 8, lambda d: mx_copy(d).start())
    blocks(lambda step, at: conv_block(
        step, lane_blocks, hq, g.sr, g.aux, g.rows, at(g.conv), at(g.q), at(g.gout), at(g.out), at(g.qs), g.fs))
    fs_eight = lambda index: pl.ds(8 * index, 8)
    fx_copy = copies(lambda d: g.fs.at[fs_eight(slab_peer(d))], lambda d: g.fs_in.at[d], (g.fx_s, g.fx_r), in_slab)
    each(1, 8, lambda d: fx_copy(d).start())
    halo.wait()
    work_back = lambda step, at: backward_block(
        me, n, g.inv, at(g.next), at(g.bspec), at(g.mspec), at(g.qs), at(g.k), at(g.v), at(g.normed), at(g.tok), at(g.prev),
        at(g.gain), g.sf.at[:, :, pl.ds(pl.multiple_of(step * width, width), width)], at(g.gskip), g.far2, g.inv_near3,
        at(g.gn), at(g.tail), g.small.at[:, :, pl.ds(pl.multiple_of(step * width, width), width)], g.dotacc, g.pads)
    blocks(work_back, 0, steps // 2)

    def add_all(copy, buffer, start, last=8):
        def body(d, now):
            copy(d).wait_recv()
            return now + buffer[d].astype(f32)

        return lax.fori_loop(1, last, body, start)

    g.slab[...] = add_all(mx_copy, g.slabs_in, g.medium[:, slab_lanes(own_slab)].astype(f32)).astype(bf16)
    taps = lambda index: pl.ds(pl.multiple_of(16 * index, 16), 16)
    mz_copy = copies(lambda d: g.slab.at[taps(z_peer(d))], lambda d: g.tiles_in.at[d], (g.mz_s, g.mz_r), in_z)
    each(1, 8, lambda d: mz_copy(d).start())
    g.fs_slab[...] = add_all(fx_copy, g.fs_in, g.fs[fs_eight(own_slab)])
    fz_copy = copies(lambda d: g.fs_slab.at[z_peer(d)], lambda d: g.fsz_in.at[d], (g.fz_s, g.fz_r), in_z)
    each(1, 8, lambda d: fz_copy(d).start())
    blocks(work_back, steps // 2, steps)

    tail_copy = near(5, g.tail, g.tail_in, peer(n - 1))
    tail_copy.start()
    sx_copy = copies(lambda d: g.small.at[:, :, slab_lanes(slab_peer(d))], lambda d: g.small_in.at[d], (g.sx_s, g.sx_r), in_slab)
    each(1, 8, lambda d: sx_copy(d).start())

    tile = add_all(mz_copy, g.tiles_in, g.slab[taps(me_z)].astype(f32)).astype(bf16)
    g.tile_red[...] = tile
    az_copy = copies(lambda d: g.tile_red, lambda d: g.slab_all.at[taps(me_z)], (g.az_s, g.az_r), in_z)
    each(1, 8, lambda d: az_copy(d).start())
    g.slab_all[taps(me_z)] = tile

    tail_copy.wait()
    extra = jnp.where(me < n - 1, g.tail_in[...], 0.0)
    gn_last = g.gn[TOK - 8:TOK] + extra
    tail_dot = jnp.sum(extra * g.gain[...] * g.tok[TOK - 16:TOK].astype(f32)[8:16], axis=1, keepdims=True)
    column = jnp.sum(g.dotacc[...], axis=1, keepdims=True)
    column = jnp.concatenate([column[:TOK - 8], column[TOK - 8:] + tail_dot], 0)
    dots = g.dots
    dots[...] = jnp.broadcast_to(to_row(column), dots.shape)
    dot_copy = lambda d: send(dots, g.dots_in.at[d], g.dot_s.at[d], g.dot_r.at[d], tp=tp_peer(d))
    for d in range(1, n_tp):
        dot_copy(d).start()

    g.small_slab[...] = add_all(sx_copy, g.small_in, g.small[:, :, slab_lanes(own_slab)])
    sz_copy = copies(lambda d: g.small_slab, lambda d: g.smallz_in.at[d], (g.sz_s, g.sz_r), in_z)
    each(1, 8, lambda d: sz_copy(d).start())

    both = add_all(fz_copy, g.fsz_in, g.fs_slab[me_z])
    pair = [g.rows[(2 * me_z + i) * 4 + me_x] for i in range(2)]
    pick_core = lambda rows_now, at: jnp.where(core == 0, rows_now[at:at + 1], rows_now[at + 1:at + 2])
    res = jnp.concatenate([pick_core(rows_now, 0) for rows_now in pair], 0)
    rate = jnp.concatenate([pick_core(rows_now, 2) for rows_now in pair], 0)
    first, second = both[0:2], both[2:4]
    root = jnp.sqrt(rate)
    fin = g.fin
    fin[0:2] = root * first
    fin[2:4] = res / length * (first / (2.0 * root) - root * second)

    def fin_to(t):
        where = me_x * row + core * 8 + t
        return where, send(fin, g.fin_all.at[me_z], g.fin_s.at[t], g.fin_r.at[me_z], ctx=where)

    def fin_from(t):
        owner = me_x * row + 2 * t + me_z // 4
        return owner, send(fin, g.fin_all.at[t], g.fin_s.at[t], g.fin_r.at[t], ctx=owner)

    def start_fin(t):
        where, copy = fin_to(t)

        @pl.when(where != me)
        def _():
            copy.start()

    each(0, 8, start_fin)

    @pl.when(core == me_z // 4)
    def _():
        g.fin_all[me_z] = fin[...]

    dot_row = dots[...]
    for d in range(1, n_tp):
        dot_copy(d).wait()
        dot_row = dot_row + g.dots_in[d]
    inv_row = g.inv[0]
    factor = to_column((inv_row * inv_row * inv_row * dot_row / total)[0:1])
    inv = to_column(inv_row[0:1])
    for block in range(lane_blocks):
        lanes = slice(block * LANES, (block + 1) * LANES)
        gn = jnp.concatenate([g.gn[0:TOK - 8, lanes], gn_last[:, lanes]], 0)
        g.gtok[:, lanes] = (inv * (gn * g.gain[:, lanes]) - g.tok[:, lanes].astype(f32) * factor).astype(bf16)

    small_sum = add_all(sz_copy, g.smallz_in, g.small_slab[...])
    g.small_sum[...] = small_sum
    bx_copy = copies(lambda d: g.small_sum, lambda d: g.small_all.at[:, :, slab_lanes(own_slab)], (g.bx_s, g.bx_r), in_slab)
    each(1, 8, lambda d: bx_copy(d).start())
    g.small_all[:, :, slab_lanes(own_slab)] = small_sum
    each(1, 8, lambda d: az_copy(d).wait_recv())
    ax_copy = copies(lambda d: g.slab_all, lambda d: g.medium_all.at[:, slab_lanes(own_slab)], (g.ax_s, g.ax_r), in_slab)
    each(1, 8, lambda d: ax_copy(d).start())
    g.medium_all[:, slab_lanes(own_slab)] = g.slab_all[...]

    def finish_fin(t):
        where, out_copy = fin_to(t)
        owner, in_copy = fin_from(t)

        @pl.when(where != me)
        def _():
            out_copy.wait_send()

        @pl.when(owner != me)
        def _():
            in_copy.wait_recv()

    def finish_eight(d):
        for copy in (mx_copy, fx_copy, mz_copy, fz_copy, az_copy, sx_copy, sz_copy):
            copy(d).wait_send()
        bx_copy(d).wait()
        ax_copy(d).wait()

    def finish_row(d):
        sr_copy(d).wait_send()
        hq_copy(d).wait_send()

    for d in range(1, n_tp):
        sum_copy(d).wait_send()
    each(1, n, lambda d: par_copy(d).wait_send())
    each(1, row, finish_row)
    each(0, 8, finish_fin)
    each(1, 8, finish_eight)


def finish_kernel(out_in, gtok_in, medium_in, small_in, fin_in, out_ref, gtok_ref, gain_ref, short_ref, medium_ref, skip_ref, res_ref, decay_ref):
    me = lax.axis_index("ctx")
    out_ref[...] = out_in[...]
    gtok_ref[...] = gtok_in[...]
    medium_ref[...] = medium_in[...].astype(f32)
    offset = 16 * lax.rem(me, 8)
    select = (lax.broadcasted_iota(jnp.int32, (16, LANES), 0) + offset == lax.broadcasted_iota(jnp.int32, (16, LANES), 1)).astype(f32)
    home = pl.multiple_of((me // 8) * LANES, LANES)
    pick = lambda left, right: lax.dot_general(left, right, (((1,), (1,)), ((), ())), precision=HIGHEST, preferred_element_type=f32)
    res_ref[...] = pick(select, jnp.concatenate([fin_in[i, 0:2] for i in range(8)], 0))
    decay_ref[...] = pick(select, jnp.concatenate([fin_in[i, 2:4] for i in range(8)], 0))
    for index in range(9):
        short_ref[index // 3, index % 3:index % 3 + 1] = small_in[index // 2, index % 2:index % 2 + 1]
    gain_ref[...] = small_in[4, 1:2]
    skip_row = small_in[5, 0:1, pl.ds(home, LANES)]
    skip_ref[...] = pick(jnp.broadcast_to(skip_row, (8, LANES)), select)[0:1]


def block_width(channels):
    return min(256, channels)


def per_device(tokens, norm_gain, short_filter, medium_filter, residues, decay_rate, skip_gain, grad_out):
    channels = tokens.shape[1]
    n, n_tp = lax.axis_size("ctx"), lax.axis_size("tp")
    width = block_width(channels)
    shape = jax.ShapeDtypeStruct
    inputs = dict(
        tok=tokens, gout=grad_out, res=residues, rate=decay_rate, skipg=skip_gain.reshape(1, -1), gain=norm_gain.reshape(1, channels),
        sf=short_filter, mf=medium_filter, order=jnp.asarray(lane_orders()),
        **{name: jnp.asarray(table) for name, table in transform_tables().items()})
    outputs = dict(
        out=shape((TOK, channels), bf16), gtok=shape((TOK, channels), bf16), medium_all=shape((TOK, channels), bf16),
        small_all=shape((8, 2, channels), f32), fin_all=shape((8, 4, LANES), f32))
    scratch = scratch_list(n, n_tp, channels, width)
    results = pl.pallas_call(
        functools.partial(main_kernel, n, n_tp, channels * n_tp, [*inputs, *outputs, *scratch]),
        out_shape=tuple(outputs.values()),
        in_specs=[VMEM_SPEC] * len(inputs),
        out_specs=[VMEM_SPEC] * len(outputs),
        scratch_shapes=list(scratch.values()),
        compiler_params=pltpu.CompilerParams(collective_id=1, has_side_effects=True),
        name="block",
    )(*inputs.values())
    small = skip_gain.shape[0]
    outs = pl.pallas_call(
        finish_kernel,
        out_shape=(shape((TOK, channels), bf16), shape((TOK, channels), bf16), shape((1, channels), f32), shape((3, 3, channels), f32),
                   shape((TOK, channels), f32), shape((1, small), f32), shape((small, MODES), f32), shape((small, MODES), f32)),
        in_specs=[VMEM_SPEC] * 5,
        out_specs=[VMEM_SPEC] * 8,
        name="finish",
    )(*results)
    block_out, grad_tokens, grad_gain, grad_short, grad_medium, grad_skip, grad_residues, grad_decay = outs
    return (block_out, grad_tokens, grad_gain.reshape(channels), grad_short, grad_medium, grad_skip.reshape(small), grad_residues, grad_decay)


def solution(mesh):
    cols = P(("tp", "ctx"), None)
    specs = (P("ctx", "tp"), P("tp"), P(None, None, "tp"), P(None, "tp"), cols, cols, P(("tp", "ctx")), P("ctx", "tp"))
    outs = (P("ctx", "tp"), P("ctx", "tp"), P("tp"), P(None, None, "tp"), P(None, "tp"), P(("tp", "ctx")), cols, cols)
    return jax.shard_map(per_device, mesh=mesh, in_specs=specs, out_specs=outs, check_vma=False)
```

time: 92.9 us -> 80.9 us (0.87)
  Pallas kernels: 92.1 us -> 80.2 us
    pallas_call x1, Pallas kernels: 89.9 us -> 78 us  [per_device(): pl.pallas_call(functools.partial(main_kernel, n, n_tp, channels * n_tp, [...]
where the time goes in v3:
time: 80.9 us; the launch traced here: 80.8 us
  Pallas kernels  80.2 us (99%)
    pallas_call x1, Pallas kernels, per_device(): pl.pallas_call(functools.partial(main_kernel, n, n_tp, channels * n_tp, [...  78 us
    pallas_call x1, Pallas kernels, per_device(): pl.pallas_call(finish_kernel, out_shape=(shape((TOK, channels), bf16), sh...  2.19 us

profile of v3, /device:TPU:1, one launch (start us, length us, event | category | flops | bytes accessed | tf_op | source)
XLA Modules:
  0.0 80.8 jit_solution(16456350937045072852)
XLA Ops:
  0.6 78.0 %block.1 = (bf16[128,1024]{1,0:T(8,128)(2,1)}, bf16[128,1024]{1,0:T(8,128)(2,1)}, bf16[128,1024]{1,0:T(8,128)(2,1)}, f32[8,2,1024]{2,1,0:T(2,128)}, f32[8,4,128]{2,1,0:T(4,128)}) custom-call(bf16[128,1024]{1,0:T(8,128)(2,1)} %refs_0_.1, bf16[128,1024]{1,0:T(8,128)(2,1)} %refs_1_.1, f32[16,16]{1,0:T(8,128)} %refs_2_.1, f32[16,16]{1,0:T(8,128)} %refs_3_.1, ...), custom_call_target="tpu_custom_call" | custom-call | tf_op jit(solution)/shard_map/block/pallas_call | solution.py:715
  78.6 2.2 %finish.1 = (bf16[128,1024]{1,0:T(8,128)(2,1)}, bf16[128,1024]{1,0:T(8,128)(2,1)}, f32[1,1024]{1,0:T(1,128)}, f32[3,3,1024]{2,1,0:T(4,128)}, f32[128,1024]{1,0:T...) custom-call(bf16[128,1024]{1,0:T(8,128)(2,1)} %get-tuple-element.21.out_in, ...), custom_call_target="tpu_custom_call" | custom-call | tf_op jit(solution)/shard_map/finish/pallas_call | solution.py:725

commit v4 on v3

--- a/solution.py
+++ b/solution.py
@@ -94,16 +94,6 @@
     if lane_blocks == 1:
         return row // 2, row % 2
     return row * (lane_blocks // 2) + step, part
-
-
-def greet(barrier, count, axis):
-    me = lax.axis_index(axis)
-
-    def body(d, carry):
-        pl.semaphore_signal(barrier, inc=1, device_id={axis: lax.rem(me + d, count)}, device_id_type=MESH)
-        return carry
-
-    lax.fori_loop(1, count, body, 0)
 
 
 def send(src, dst, send_sem, recv_sem, **where):
@@ -347,7 +337,7 @@
     dma = lambda *shape: pltpu.SemaphoreType.DMA(shape)
     entries = dict(
         inv=pltpu.VMEM((3, 8, TOK), f32), prev=wide(TOK, bf16), prev2=wide(16, bf16), par=piece(8),
-        msg=pltpu.VMEM((8, LANES), f32), sums=row_tile, sums_in=pltpu.VMEM((n_tp, 8, TOK), f32), inv_own=row_tile,
+        msg=pltpu.VMEM((8, LANES), f32), sums=row_tile, sums_in=pltpu.VMEM((3, n_tp, 8, TOK), f32),
         q=wide(TOK), k=wide(TOK), v=wide(TOK), normed=wide(136), gspec=wide(256), mspec=wide(256), bspec=wide(256),
         sig=wide(TOK), grd=wide(TOK), conv=wide(TOK), backl=wide(TOK), gskip=wide(1), skip=wide(1),
         sr=piece(4), aux=piece(8), rows=piece(8), inbox=piece(4), outbox=piece(4), hq=piece(4),
@@ -361,11 +351,11 @@
         gn=wide(TOK), tail=wide(8), tail_in=wide(8),
         dotacc=pltpu.VMEM((TOK, LANES), f32), dots=row_tile, dots_in=pltpu.VMEM((n_tp, 8, TOK), f32),
         ext=pltpu.VMEM((272, width), f32), kern=pltpu.VMEM((TOK, width), f32), kgr=pltpu.VMEM((TOK, width), f32), pads=pltpu.VMEM((3, 144, width), f32),
-        par_s=dma(n), par_r=dma(n), sr_s=dma(16), sr_r=dma(16), hq_s=dma(16), hq_r=dma(16), tot_s=dma(NX), tot_r=dma(NX),
+        par_s=dma(16), par_r=dma(16), parx_s=dma(NX), parx_r=dma(NX), sr_s=dma(16), sr_r=dma(16), hq_s=dma(16), hq_r=dma(16), tot_s=dma(NX), tot_r=dma(NX),
         mx_s=dma(8), mx_r=dma(8), mz_s=dma(8), mz_r=dma(8), az_s=dma(8), az_r=dma(8), ax_s=dma(8), ax_r=dma(8),
         fx_s=dma(8), fx_r=dma(8), fz_s=dma(8), fz_r=dma(8), fin_s=dma(8), fin_r=dma(8),
         sx_s=dma(8), sx_r=dma(8), sz_s=dma(8), sz_r=dma(8), bx_s=dma(8), bx_r=dma(8),
-        sum_s=dma(n_tp), sum_r=dma(n_tp), dot_s=dma(n_tp), dot_r=dma(n_tp), near_s=dma(6), near_r=dma(6),
+        sum_s=dma(3 * n_tp), sum_r=dma(3 * n_tp), dot_s=dma(n_tp), dot_r=dma(n_tp), near_s=dma(6), near_r=dma(6),
     )
     return entries
 
@@ -433,8 +423,19 @@
         return send(source, target, g.near_s.at[index], g.near_r.at[index], ctx=where)
 
     barrier = pltpu.get_barrier_semaphore()
-    greet(barrier, n, "ctx")
-    greet(barrier, n_tp, "tp")
+
+    def tell(**where):
+        pl.semaphore_signal(barrier, inc=1, device_id=where, device_id_type=MESH)
+
+    each(1, row, lambda d: tell(ctx=in_row(d)))
+    each(1, 8, lambda d: tell(ctx=in_slab(d)))
+    for d in range(n_tp):
+        if d:
+            tell(tp=tp_peer(d))
+        tell(ctx=peer(n - 1), tp=tp_peer(d))
+        tell(ctx=peer(n - 2), tp=tp_peer(d))
+    tell(ctx=peer(1))
+    expected = row - 1 + 7 + 3 * n_tp
     length = n * TOK
     msg = g.msg
     msg[...] = jnp.zeros(msg.shape, f32)
@@ -455,36 +456,43 @@
         at(g.mspec)[...] = dot3(g.near3[...], at(g.mf)[...])
 
     blocks(filter_spectrum)
-    pl.semaphore_wait(barrier, n - 1 + n_tp - 1)
-
-    sum_copy = lambda d: send(sums, g.sums_in.at[d], g.sum_s.at[d], g.sum_r.at[d], tp=tp_peer(d))
-    par_copy = copies(lambda d: msg, lambda d: g.par.at[me], (g.par_s, g.par_r))
+    pl.semaphore_wait(barrier, expected)
+
+    sum_pairs = [(e, d) for e in range(3) for d in range(n_tp) if e or d]
+
+    def sum_copy(e, d):
+        return send(sums, g.sums_in.at[e, d], g.sum_s.at[n_tp * e + d], g.sum_r.at[n_tp * e + d], ctx=peer(e), tp=tp_peer(d))
+
+    par_copy = copies(lambda d: msg, lambda d: g.par.at[me], (g.par_s, g.par_r), in_row)
+    own_row = pl.ds(me_x * row, row)
+    parx_copy = copies(lambda d: g.par.at[own_row], lambda d: g.par.at[own_row], (g.parx_s, g.parx_r), in_x)
     tok_copy = near(0, g.tok, g.prev, peer(1))
     tok2_copy = near(1, g.tok.at[pl.ds(TOK - 16, 16)], g.prev2, peer(2))
-    for d in range(1, n_tp):
-        sum_copy(d).start()
+    for e, d in sum_pairs:
+        sum_copy(e, d).start()
     tok2_copy.start()
+    each(1, row, lambda d: par_copy(d).start())
     tok_copy.start()
-    each(1, n, lambda d: par_copy(d).start())
     g.par[me] = msg[...]
-    squares = sums[...]
-    for d in range(1, n_tp):
-        sum_copy(d).wait_recv()
-        squares = squares + g.sums_in[d]
-    inv_own = g.inv_own
-    inv_own[...] = lax.rsqrt(squares / total + EPSILON)
-    inv_copies = [near(2, inv_own, g.inv.at[1], peer(1)), near(3, inv_own, g.inv.at[2], peer(2))]
-    for copy in inv_copies:
-        copy.start()
-    g.inv[0] = inv_own[...]
-    for copy in inv_copies + [tok_copy, tok2_copy]:
-        copy.wait()
+    for e in range(3):
+        squares = sums[...] if e == 0 else jnp.zeros(sums.shape, f32)
+        for d in range(n_tp):
+            if e or d:
+                sum_copy(e, d).wait_recv()
+                squares = squares + g.sums_in[e, d]
+        g.inv[e] = lax.rsqrt(squares / total + EPSILON)
+    each(1, row, lambda d: par_copy(d).wait_recv())
+    for d in range(1, NX):
+        parx_copy(d).start()
+    tok2_copy.wait()
+    tok_copy.wait()
 
     blocks(lambda step, at: signals_block(
         me, g.inv, at(g.tok), at(g.prev), at(g.prev2), at(g.gain), g.sf.at[:, :, pl.ds(pl.multiple_of(step * width, width), width)], at(g.gout),
         g.whole2, g.inv_far3, at(g.q), at(g.k), at(g.v), at(g.normed), at(g.gspec), at(g.mspec), at(g.gskip), at(g.sig), at(g.grd), g.ext))
 
-    each(1, n, lambda d: par_copy(d).wait_recv())
+    for d in range(1, NX):
+        parx_copy(d).wait_recv()
     blocks(lambda step, at: sums_block(
         step, lane_blocks, g.par.at[pl.ds(step * (8 * width // LANES), 8 * width // LANES)], g.order, at(g.sig), at(g.grd), g.sr, g.aux, g.rows, at(g.skip)))
     inbox, outbox, hq = g.inbox, g.outbox, g.hq
@@ -666,12 +674,14 @@
         ax_copy(d).wait()
 
     def finish_row(d):
+        par_copy(d).wait_send()
         sr_copy(d).wait_send()
         hq_copy(d).wait_send()
 
-    for d in range(1, n_tp):
-        sum_copy(d).wait_send()
-    each(1, n, lambda d: par_copy(d).wait_send())
+    for e, d in sum_pairs:
+        sum_copy(e, d).wait_send()
+    for d in range(1, NX):
+        parx_copy(d).wait_send()
     each(1, row, finish_row)
     each(0, 8, finish_fin)
     each(1, 8, finish_eight)

time: 80.9 us -> 76.1 us (0.941)
  Pallas kernels: 80.2 us -> 75.3 us
    pallas_call x1, Pallas kernels: 78 us -> 73.2 us  [per_device(): pl.pallas_call(functools.partial(main_kernel, n, n_tp, channels * n_tp, [...]
where the time goes in v4:
time: 76.1 us; the launch traced here: 76 us
  Pallas kernels  75.3 us (99%)
    pallas_call x1, Pallas kernels, per_device(): pl.pallas_call(functools.partial(main_kernel, n, n_tp, channels * n_tp, [...  73.2 us
    pallas_call x1, Pallas kernels, per_device(): pl.pallas_call(finish_kernel, out_shape=(shape((TOK, channels), bf16), sh...  2.19 us

profile of v4, /device:TPU:1, one launch (start us, length us, event | category | flops | bytes accessed | tf_op | source)
XLA Modules:
  0.0 76.0 jit_solution(618151092807571950)
XLA Ops:
  0.6 73.2 %block.1 = (bf16[128,1024]{1,0:T(8,128)(2,1)}, bf16[128,1024]{1,0:T(8,128)(2,1)}, bf16[128,1024]{1,0:T(8,128)(2,1)}, f32[8,2,1024]{2,1,0:T(2,128)}, f32[8,4,128]{2,1,0:T(4,128)}) custom-call(bf16[128,1024]{1,0:T(8,128)(2,1)} %refs_0_.1, bf16[128,1024]{1,0:T(8,128)(2,1)} %refs_1_.1, f32[16,16]{1,0:T(8,128)} %refs_2_.1, f32[16,16]{1,0:T(8,128)} %refs_3_.1, ...), custom_call_target="tpu_custom_call" | custom-call | tf_op jit(solution)/shard_map/block/pallas_call | solution.py:725
  73.8 2.2 %finish.1 = (bf16[128,1024]{1,0:T(8,128)(2,1)}, bf16[128,1024]{1,0:T(8,128)(2,1)}, f32[1,1024]{1,0:T(1,128)}, f32[3,3,1024]{2,1,0:T(4,128)}, f32[128,1024]{1,0:T...) custom-call(bf16[128,1024]{1,0:T(8,128)(2,1)} %get-tuple-element.21.out_in, ...), custom_call_target="tpu_custom_call" | custom-call | tf_op jit(solution)/shard_map/finish/pallas_call | solution.py:735
